TPU v7x, 256 devices: a whole 4x4x8 slice. The times are simulated.
256 devices in a mesh: wide: 64 (over y, z, core), narrow: 4 (over x).
Axes of the slice: x: 4, y: 4, z: 8, core: 2. Of those that a mesh axis runs over, the one named last changes fastest.
Arguments:
- features: bfloat16 [768, 524288], P('narrow', 'wide'), may hold values from -6 to 6
- owner_of: int32 [32768, 16, 1], P('wide'), may hold values from 0 to 63; in each aligned block of 8192 rows (0 to 8191, 8192 to 16383, ..., all dimensions but the last counted through in order) at most 192 rows name the same one
- row_of: int32 [32768, 16], P('wide'), may hold values from 0 to 8191
- w_self: bfloat16 [768, 256], P('narrow'), may hold values from -0.15625 to 0.15625
- w_neighbor: bfloat16 [768, 256], P('narrow'), may hold values from -0.15625 to 0.15625
- cotangent: bfloat16 [32768, 256], P(('wide', 'narrow')), may hold values from -0.032958984 to 0.032958984
Outputs:
- hidden: bfloat16 [32768, 256], P(('wide', 'narrow'))
- grad_self: float32 [768, 256], P('narrow')
- grad_neighbor: float32 [768, 256], P('narrow')
Inputs may be any that keep to these rules, and one draw needn't show every extreme that they name: `owner_of`: among the 8192 rows read by the targets of one index of wide, no owner is named more than 192 times, and in every draw some owner is named exactly 192 times by some index.
All inputs are finite; a program needn't handle non-finite values.
Results may differ from a plain program's by a relative error of at most 0.0054.
Values may be sent and summed in bfloat16 or wider, within the bound.
A program may use at most 64 MiB of HBM per device.

v0:
```python
import jax
import jax.numpy as jnp
from jax import lax
from jax.sharding import PartitionSpec as P

FANOUT = 15


def activation(value):
    return jax.nn.gelu(value, approximate=True)


def contract_rows(left, right):
    return lax.dot_general(
        left, right, (((0,), (0,)), ((), ())), preferred_element_type=jnp.float32
    )


def slot_numbers(owners, wide_count, total):
    block_rows = 128
    block_count = total // block_rows
    onehot = (owners[:, None] == jnp.arange(wide_count, dtype=jnp.int32)[None, :]).astype(
        jnp.float32
    )
    blocked = onehot.reshape(block_count, block_rows, wide_count)
    lower = (jnp.arange(block_rows)[:, None] > jnp.arange(block_rows)[None, :]).astype(jnp.float32)
    within = jnp.einsum("ij,bjw->biw", lower, blocked, precision=lax.Precision.HIGHEST)
    block_sums = jnp.sum(blocked, axis=1)
    offsets = jnp.cumsum(block_sums, axis=0) - block_sums
    prefix = within + offsets[:, None, :]
    return jnp.sum(prefix * blocked, axis=2).reshape(total).astype(jnp.int32)


def on_device(features, owner_of, row_of, w_self, w_neighbor, cotangent):
    wide_count = lax.axis_size("wide")
    narrow_count = lax.axis_size("narrow")
    tgt_rows, request_count = row_of.shape
    feat_cols = features.shape[0]
    total = tgt_rows * request_count
    capacity = max(2, 3 * total // (2 * wide_count))
    owners = owner_of.reshape(total)
    wanted = row_of.reshape(total)
    slot_of = slot_numbers(owners, wide_count, total)
    flat_slot = owners * capacity + slot_of
    buffer = (
        jnp.zeros((wide_count * capacity,), jnp.int32)
        .at[flat_slot]
        .set(wanted)
        .reshape(wide_count, capacity)
    )
    table = jnp.transpose(features)
    found = jnp.take(
        table, lax.all_to_all(buffer, "wide", split_axis=0, concat_axis=0, tiled=True), axis=0
    )
    fetched = lax.all_to_all(found, "wide", split_axis=0, concat_axis=0, tiled=True)
    flat_fetched = fetched.reshape(wide_count * capacity, feat_cols)
    gathered = jnp.take(flat_fetched, flat_slot, axis=0).reshape(tgt_rows, request_count, feat_cols)
    self_rows = gathered[:, 0]
    pooled = (jnp.sum(gathered[:, 1:], axis=1, dtype=jnp.float32) / FANOUT).astype(jnp.bfloat16)
    share = tgt_rows // narrow_count
    preact = lax.psum(
        jnp.dot(self_rows, w_self, preferred_element_type=jnp.float32)
        + jnp.dot(pooled, w_neighbor, preferred_element_type=jnp.float32),
        "narrow",
    )
    value, pullback = jax.vjp(activation, preact)
    full_cot = lax.all_gather(cotangent, "narrow", axis=0, tiled=True)
    slope = pullback(full_cot.astype(jnp.float32))[0].astype(jnp.bfloat16)
    mine = lax.axis_index("narrow") * share
    hidden = lax.dynamic_slice_in_dim(value, mine, share, 0).astype(jnp.bfloat16)
    grad_self, grad_neighbor = lax.psum(
        (contract_rows(self_rows, slope), contract_rows(pooled, slope)), "wide"
    )
    return (hidden, grad_self, grad_neighbor)


def solution(mesh):
    return jax.shard_map(
        on_device,
        mesh=mesh,
        in_specs=(
            P("narrow", "wide"),
            P("wide", None, None),
            P("wide", None),
            P("narrow", None),
            P("narrow", None),
            P(("wide", "narrow"), None),
        ),
        out_specs=(P(("wide", "narrow"), None), P("narrow", None), P("narrow", None)),
        check_vma=False,
    )
```

profile of v0, /device:TPU:1, one launch (start us, length us, event | category | flops | bytes accessed | tf_op | source)
XLA Modules:
  0.0 561.1 jit_solution(12965184154446572540)
XLA Ops:
  7.2 0.0 copy-start
  7.2 0.0 copy-start.2
  7.2 1.0 copy.24
  8.2 1.4 copy_multiply_fusion
  9.6 0.1 eq.17
  9.7 0.6 convert_reduce_fusion.1
  10.4 0.1 reduce_window_sum.11
  10.5 0.8 fusion
  11.3 0.9 copy.26
  12.2 0.8 mul.76
  13.0 0.9 copy.27
  13.9 0.7 reshape.155
  14.6 0.8 compare_select_fusion.1
  15.4 30.7 %scatter_custom_fusion = s32[12288]{0:T(1024)S(1)} fusion(s32[8192]{0:T(1024)S(1)} %bitcast.41, s32[8192]{0:T(1024)} %reshape.155, s32[]{:T(128)} %constant.21.clone.1), kind=kCustom, calls=%fused_computation.47 | custom fusion | bytes 49664 | tf_op jit(solution)/shard_map/scatter | solution.py:48
  46.1 0.8 all_to_all.13
  46.9 13.1 %all-to-all-start = ((s32[64,1,192]{2,1,0:T(1,128)}), s32[64,1,192]{2,1,0:T(1,128)S(1)}, u32[]{:S(2)}, u32[]{:S(2)}) async-start(s32[64,1,192]{2,1,0:T(1,128)} %all_to_all.13), calls=%async_computation | async-start | bytes 131072 | tf_op jit(solution)/shard_map/all_to_all | solution.py:53
  60.0 0.0 copy-done.2
  60.0 4.0 copy.28
  64.0 5.8 %all-to-all-done = s32[64,1,192]{2,1,0:T(1,128)S(1)} async-done(((s32[64,1,192]{2,1,0:T(1,128)}), s32[64,1,192]{2,1,0:T(1,128)S(1)}, u32[]{:S(2)}, u32[]{:S(2)}) %all-to-all-start) | async-done | bytes 49184 | tf_op jit(solution)/shard_map/all_to_all | solution.py:53
  69.8 0.2 fusion.17
  70.0 0.1 reshape.137
  70.1 48.5 %gather_fusion = bf16[12288,192]{1,0:T(8,128)(2,1)} fusion(bf16[8192,192]{1,0:T(8,128)(2,1)} %bitcast.37, s32[12288]{0:T(1024)S(1)} %broadcast_clamp_fusion), kind=kCustom, calls=%fused_computation | custom fusion | bytes 9486336 | tf_op jit(solution)/shard_map/jit(_take)/gather | solution.py:52
  118.7 7.6 %broadcast_select_fusion = bf16[64,192,192]{2,1,0:T(8,128)(2,1)} fusion(bf16[64,192,192]{2,1,0:T(8,128)(2,1)} %bitcast.38, pred[64,192]{1,0:T(8,128)(4,1)S(1)} %compare_and_fusion), kind=kLoop, calls=%fused_computation.3 | loop fusion | flops 2359296 | bytes 9449472 | tf_op jit(solution)/shard_map/jit(_take)/select_n | solution.py:52
  126.3 0.0 copy-start.3
  126.3 5.6 all-to-all-start.1
  131.9 0.0 all-reduce.4.cloned.1.call-start
  131.9 0.1 convert_element_type.41
  132.1 0.1 copy.25
  132.2 0.0 copy-done.3
  132.2 140.5 %all-to-all-done.1 = bf16[64,192,192]{2,1,0:T(8,128)(2,1)} async-done(((bf16[64,192,192]{2,1,0:T(8,128)(2,1)}), bf16[64,192,192]{2,1,0:T(8,128)(2,1)}, u32[]{:S(2)}, u32[]{:S(2)}) %all-to-all-start.1) | async-done | bytes 4718624 | tf_op jit(solution)/shard_map/all_to_all | solution.py:55
  272.8 34.5 %gather_fusion.1 = bf16[8192,192]{1,0:T(8,128)(2,1)} fusion(bf16[12288,192]{1,0:T(8,128)(2,1)} %bitcast.8, s32[8192]{0:T(1024)S(1)} %broadcast_clamp_fusion.1), kind=kCustom, calls=%fused_computation.1 | custom fusion | bytes 6324224 | tf_op jit(solution)/shard_map/jit(_take)/gather | solution.py:57
  307.2 7.7 %copy.29 = bf16[512,16,192]{0,2,1:T(8,128)(2,1)} copy(bf16[512,16,192]{2,1,0:T(8,128)(2,1)} %bitcast.39) | data formatting | bytes 6291456 | tf_op jit(solution)/shard_map/jit(_take)/gather | solution.py:57
  315.0 2.2 broadcast_select_fusion.1
  317.2 0.0 copy-start.4
  317.2 0.4 convert_reduce_fusion
  317.6 0.0 copy-done
  317.6 0.0 copy-start.1
  317.6 0.3 fusion.14
  317.9 0.5 copy-done.1
  318.3 0.0 copy-done.4
  318.3 1.1 convolution_add_fusion
  319.4 0.0 all-reduce.4.cloned.1.call-update
  319.5 0.0 all-reduce.6.cloned.1.call-start
  319.5 10.0 %all_gather.3 = bf16[512,256]{1,0:T(8,128)(2,1)S(1)} all-gather(bf16[128,256]{1,0:T(8,128)(2,1)} %param.11), channel_id=1, replica_groups=mesh['wide'=64,'narrow'=4] {'narrow'}, dimensions={0}, use_global_device_ids=true | all-gather | bytes 327680 | tf_op jit(solution)/shard_map/all_gather | solution.py:67
  329.5 32.6 %all-reduce.4.cloned.1.call-done = f32[512,256]{1,0:T(8,128)} async-done(((f32[512,256]{1,0:T(8,128)}), f32[512,256]{1,0:T(8,128)}) %all-reduce.4.cloned.1.call-update) | async-done | bytes 524304 | tf_op jit(solution)/shard_map/psum | solution.py:61
  362.1 2.2 fusion.5
  364.3 1.9 fusion.16
  366.2 0.9 fusion.13
  367.1 0.0 all-reduce.6.cloned.1.call-update
  367.1 1.6 fusion.15
  368.7 182.3 %all-reduce.6.cloned.1.call-done = (f32[192,256]{1,0:T(8,128)}, f32[192,256]{1,0:T(8,128)}) async-done(((f32[192,256]{1,0:T(8,128)}, f32[192,256]{1,0:T(8,128)}), (f32[192,256]{1,0:T(8,128)}, f32[192,256]{1,0:T(8,128)})) %all-reduce.6.cloned.1.call-update) | async-done | bytes 393232 | tf_op jit(solution)/shard_map/psum | solution.py:71
  551.1 1.6 copy.40
  552.7 1.6 copy.41
  (6 shorter events, 0.1 us)
Async XLA Ops:
  7.2 310.4 %copy-start = (bf16[192,256]{1,0:T(8,128)(2,1)S(1)}, bf16[192,256]{1,0:T(8,128)(2,1)}, u32[]{:S(2)}) copy-start(bf16[192,256]{1,0:T(8,128)(2,1)} %param.9) | copy-start | bytes 294916
  7.2 52.8 %copy-start.2 = (bf16[192,8192]{1,0:T(8,128)(2,1)S(1)}, bf16[192,8192]{1,0:T(8,128)(2,1)}, u32[]{:S(2)}) copy-start(bf16[192,8192]{1,0:T(8,128)(2,1)} %param.6) | copy-start | bytes 9437188
  46.9 22.9 %all-to-all-start = ((s32[64,1,192]{2,1,0:T(1,128)}), s32[64,1,192]{2,1,0:T(1,128)S(1)}, u32[]{:S(2)}, u32[]{:S(2)}) async-start(s32[64,1,192]{2,1,0:T(1,128)} %all_to_all.13), calls=%async_computation | async-start | bytes 131072 | tf_op jit(solution)/shard_map/all_to_all | solution.py:53
  126.3 5.9 %copy-start.3 = (s32[512,16,1]{0,2,1:T(1,128)S(1)}, s32[512,16,1]{0,2,1:T(1,128)}, u32[]{:S(2)}) copy-start(s32[512,16,1]{0,2,1:T(1,128)} %param.7) | copy-start | bytes 98308
  126.3 146.5 %all-to-all-start.1 = ((bf16[64,192,192]{2,1,0:T(8,128)(2,1)}), bf16[64,192,192]{2,1,0:T(8,128)(2,1)}, u32[]{:S(2)}, u32[]{:S(2)}) async-start(bf16[64,192,192]{2,1,0:T(8,128)(2,1)} %broadcast_select_fusion), calls=%async_computation.1 | async-start | bytes 12582912 | tf_op jit(solution)/shard_map/all_to_all | solution.py:55
  131.9 230.2 %all-reduce.4.cloned.1.call-start = ((), (), s32[]{:S(2)}) async-start(), calls=%async_computation.2 | async-start | bytes 1048576 | tf_op jit(solution)/shard_map/psum | solution.py:61
  317.2 1.2 copy-start.4
  317.6 0.7 copy-start.1
  319.5 231.6 %all-reduce.6.cloned.1.call-start = ((), (), s32[]{:S(2)}) async-start(), calls=%async_computation.3 | async-start | bytes 786432 | tf_op jit(solution)/shard_map/psum | solution.py:71
Sparse Core Ops, SparseCore 0:
  319.6 42.4 all-reduce.3
  367.2 183.7 all-reduce.5
where the time goes:
time: 563 us; the launch traced here: 561 us
  waiting for transfers between devices  361 us (64%)
  local copies, waits for them, and re-layouts  135 us (24%)
  starting transfers between devices  18.8 us (3%)
  other arithmetic  17.3 us (3%)
  between operations  14.2 us (3%)
  blocking collectives  9.96 us (2%)
    psum x1, waiting for transfers between devices, on_device(): lax.psum((contract_rows(self_rows, slope), contract_rows(pooled, slope)),...  182 us
    all_to_all x1, waiting for transfers between devices, on_device(): lax.all_to_all(found, 'wide', split_axis=0, concat_axis=0, tiled=True)  141 us
    gather x1, local copies, waits for them, and re-layouts, on_device(): jnp.take(table, lax.all_to_all(buffer, 'wide', split_axis=0, concat_axis=...  48.5 us
    gather x2, local copies, waits for them, and re-layouts, on_device(): jnp.take(flat_fetched, flat_slot, axis=0)  42.2 us
    psum x1, waiting for transfers between devices, on_device(): lax.psum(jnp.dot(self_rows, w_self, preferred_element_type=jnp.float32) +...  32.6 us
    scatter x1, local copies, waits for them, and re-layouts, on_device(): buffer = jnp.zeros((wide_count * capacity,), jnp.int32).at[flat_slot].set...  30.7 us
    all_to_all x1, starting transfers between devices, on_device(): lax.all_to_all(buffer, 'wide', split_axis=0, concat_axis=0, tiled=True)  13.1 us
  transfers between devices with their start and end apart: 4, of which 4 were waited for; matrix products, arithmetic and copies ran while one was open for 1% of the time, Pallas kernels for 0%

commit v1 on v0

--- a/solution.py
+++ b/solution.py
@@ -1,19 +1,153 @@
 import jax
 import jax.numpy as jnp
 from jax import lax
+from jax.experimental import pallas as pl
+from jax.experimental.pallas import tpu as pltpu
 from jax.sharding import PartitionSpec as P
 
 FANOUT = 15
-
-
-def activation(value):
-    return jax.nn.gelu(value, approximate=True)
-
-
-def contract_rows(left, right):
-    return lax.dot_general(
-        left, right, (((0,), (0,)), ((), ())), preferred_element_type=jnp.float32
-    )
+NX, NY, NZ = 4, 4, 8
+ROOT, CUBE = 0.7978845608, 0.044715
+
+
+def remote(src, dst, send, recv, target):
+    return pltpu.make_async_remote_copy(
+        src_ref=src,
+        dst_ref=dst,
+        send_sem=send,
+        recv_sem=recv,
+        device_id=target,
+        device_id_type=pl.DeviceIdType.MESH,
+    )
+
+
+def place():
+    wide = lax.axis_index("wide")
+    return wide // 16, lax.rem(wide // 2, 8), lax.rem(wide, 2), lax.axis_index("narrow")
+
+
+def wide_at(y, z, core):
+    return (y * 8 + z) * 2 + core
+
+
+def greet(targets):
+    barrier = pltpu.get_barrier_semaphore()
+    for target in targets:
+        pl.semaphore_signal(barrier, inc=1, device_id=target, device_id_type=pl.DeviceIdType.MESH)
+    pl.semaphore_wait(barrier, len(targets))
+
+
+def tail_kernel(
+    rows_ref, w_ref, cot_ref, hid_ref, gs_ref, gn_ref,
+    part, got_part, slopes, grads, got_core, got_z, got_y, full, final,
+    x_send, x_recv, s_send, s_recv, c_send, c_recv, z_send, z_recv, y_send, y_recv, a_send, a_recv, d_send, d_recv,
+):
+    y, z, core, x = place()
+    near_x = [{"wide": wide_at(y, z, core), "narrow": lax.rem(x + k, NX)} for k in range(1, NX)]
+    near_c = {"wide": wide_at(y, z, 1 - core), "narrow": x}
+    near_z = [{"wide": wide_at(y, lax.rem(z + k, NZ), core), "narrow": x} for k in range(1, NZ)]
+    near_y = [{"wide": wide_at(lax.rem(y + k, NY), z, core), "narrow": x} for k in range(1, NY)]
+    greet(near_x + [near_c] + near_z + near_y)
+
+    for k in range(NX):
+        part[k] = jnp.dot(rows_ref[k * 128:(k + 1) * 128], w_ref[...], preferred_element_type=jnp.float32)
+    sent = []
+    for k in range(1, NX):
+        copy = remote(part.at[lax.rem(x + k, NX)], got_part.at[k - 1], x_send.at[k - 1], x_recv.at[k - 1], near_x[k - 1])
+        copy.start()
+        sent.append(copy)
+    value = part[x]
+    for k in range(1, NX):
+        sent[k - 1].wait_recv()
+        value = value + got_part[k - 1]
+    bend = jnp.tanh(ROOT * (value + CUBE * value * value * value))
+    hid_ref[...] = (0.5 * value * (1.0 + bend)).astype(jnp.bfloat16)
+    rise = 0.5 * (1.0 + bend) + 0.5 * value * (1.0 - bend * bend) * ROOT * (1.0 + 3.0 * CUBE * value * value)
+    slopes[x] = (cot_ref[...].astype(jnp.float32) * rise).astype(jnp.bfloat16)
+    for k in range(1, NX):
+        copy = remote(slopes.at[x], slopes.at[x], s_send.at[k - 1], s_recv.at[k - 1], near_x[k - 1])
+        copy.start()
+        sent.append(copy)
+    for k in range(1, NX):
+        remote(slopes.at[x], slopes.at[lax.rem(x + NX - k, NX)], s_send.at[k - 1], s_recv.at[k - 1], near_x[k - 1]).wait_recv()
+    total = jnp.zeros((384, 256), jnp.float32)
+    for k in range(NX):
+        total = total + lax.dot_general(
+            rows_ref[k * 128:(k + 1) * 128], slopes[k], (((0,), (0,)), ((), ())), preferred_element_type=jnp.float32
+        )
+    grads[...] = total.reshape(2, NZ, 24, 256)
+    copy = remote(grads.at[1 - core], got_core, c_send, c_recv, near_c)
+    copy.start()
+    sent.append(copy)
+    copy.wait_recv()
+    full[core] = grads[core] + got_core[...]
+    mine = full[core, z]
+    for k in range(1, NZ):
+        there = lax.rem(z + k, NZ)
+        copy = remote(full.at[core, there], got_z.at[k - 1], z_send.at[k - 1], z_recv.at[k - 1], near_z[k - 1])
+        copy.start()
+        sent.append(copy)
+    for k in range(1, NZ):
+        remote(full.at[core, z], got_z.at[k - 1], z_send.at[k - 1], z_recv.at[k - 1], near_z[k - 1]).wait_recv()
+        mine = mine + got_z[k - 1]
+    got_y[y] = mine
+    for k in range(1, NY):
+        copy = remote(got_y.at[y], got_y.at[y], y_send.at[k - 1], y_recv.at[k - 1], near_y[k - 1])
+        copy.start()
+        sent.append(copy)
+    for k in range(1, NY):
+        remote(got_y.at[y], got_y.at[lax.rem(y + NY - k, NY)], y_send.at[k - 1], y_recv.at[k - 1], near_y[k - 1]).wait_recv()
+    for copy in sent:
+        copy.wait_send()
+    final[core, z] = got_y[0] + got_y[1] + got_y[2] + got_y[3]
+    last = []
+    for k in range(1, NZ):
+        copy = remote(final.at[core, z], final.at[core, z], a_send.at[k - 1], a_recv.at[k - 1], near_z[k - 1])
+        copy.start()
+        last.append(copy)
+    for k in range(1, NZ):
+        remote(final.at[core, z], final.at[core, lax.rem(z + NZ - k, NZ)], a_send.at[k - 1], a_recv.at[k - 1], near_z[k - 1]).wait_recv()
+    copy = remote(final.at[core], final.at[core], d_send, d_recv, near_c)
+    copy.start()
+    last.append(copy)
+    remote(final.at[core], final.at[1 - core], d_send, d_recv, near_c).wait_recv()
+    for copy in last:
+        copy.wait_send()
+    whole = final[...].reshape(384, 256)
+    gs_ref[...] = whole[:192]
+    gn_ref[0:128] = whole[256:]
+    gn_ref[128:192] = whole[192:256]
+
+
+def tail(rows, weights, cotangent):
+    vmem = pl.BlockSpec(memory_space=pltpu.VMEM)
+    dma = pltpu.SemaphoreType.DMA
+    return pl.pallas_call(
+        tail_kernel,
+        out_shape=(
+            jax.ShapeDtypeStruct((128, 256), jnp.bfloat16),
+            jax.ShapeDtypeStruct((192, 256), jnp.float32),
+            jax.ShapeDtypeStruct((192, 256), jnp.float32),
+        ),
+        in_specs=[vmem] * 3,
+        out_specs=(vmem, vmem, vmem),
+        scratch_shapes=[
+            pltpu.VMEM((NX, 128, 256), jnp.float32),
+            pltpu.VMEM((NX - 1, 128, 256), jnp.float32),
+            pltpu.VMEM((NX, 128, 256), jnp.bfloat16),
+            pltpu.VMEM((2, NZ, 24, 256), jnp.float32),
+            pltpu.VMEM((NZ, 24, 256), jnp.float32),
+            pltpu.VMEM((NZ - 1, 24, 256), jnp.float32),
+            pltpu.VMEM((NY, 24, 256), jnp.float32),
+            pltpu.VMEM((2, NZ, 24, 256), jnp.float32),
+            pltpu.VMEM((2, NZ, 24, 256), jnp.float32),
+            dma((NX - 1,)), dma((NX - 1,)), dma((NX - 1,)), dma((NX - 1,)), dma(()), dma(()),
+            dma((NZ - 1,)), dma((NZ - 1,)), dma((NY - 1,)), dma((NY - 1,)),
+            dma((NZ - 1,)), dma((NZ - 1,)), dma(()), dma(()),
+        ],
+        compiler_params=pltpu.CompilerParams(collective_id=3, has_side_effects=True),
+        name="tail",
+    )(rows, weights, cotangent)
 
 
 def slot_numbers(owners, wide_count, total):
@@ -57,21 +191,9 @@
     gathered = jnp.take(flat_fetched, flat_slot, axis=0).reshape(tgt_rows, request_count, feat_cols)
     self_rows = gathered[:, 0]
     pooled = (jnp.sum(gathered[:, 1:], axis=1, dtype=jnp.float32) / FANOUT).astype(jnp.bfloat16)
-    share = tgt_rows // narrow_count
-    preact = lax.psum(
-        jnp.dot(self_rows, w_self, preferred_element_type=jnp.float32)
-        + jnp.dot(pooled, w_neighbor, preferred_element_type=jnp.float32),
-        "narrow",
-    )
-    value, pullback = jax.vjp(activation, preact)
-    full_cot = lax.all_gather(cotangent, "narrow", axis=0, tiled=True)
-    slope = pullback(full_cot.astype(jnp.float32))[0].astype(jnp.bfloat16)
-    mine = lax.axis_index("narrow") * share
-    hidden = lax.dynamic_slice_in_dim(value, mine, share, 0).astype(jnp.bfloat16)
-    grad_self, grad_neighbor = lax.psum(
-        (contract_rows(self_rows, slope), contract_rows(pooled, slope)), "wide"
-    )
-    return (hidden, grad_self, grad_neighbor)
+    rows = jnp.concatenate([self_rows, pooled[:, 128:], pooled[:, :128]], axis=1)
+    weights = jnp.concatenate([w_self, w_neighbor[128:], w_neighbor[:128]], axis=0)
+    return tail(rows, weights, cotangent)
 
 
 def solution(mesh):

time: 563 us -> 348 us (0.62)
  waiting for transfers between devices: 361 us -> 146 us
  Pallas kernels: 0 us -> 40.4 us
  between operations: 14.2 us -> 0.88 us
  local copies, waits for them, and re-layouts: 135 us -> 125 us
  blocking collectives: 9.96 us -> 0 us
    psum x2 -> x0, waiting for transfers between devices: 215 us -> none  [the longest x1 182 us: on_device(): lax.psum((contract_rows(self_rows, slope), contract_rows(pooled, slope)),...]
    pallas_call x0 -> x1, Pallas kernels: none -> 40.4 us  [tail(): pl.pallas_call(tail_kernel, out_shape=(jax.ShapeDtypeStruct((128, 256), j...]
    all_gather x1 -> x0, blocking collectives: 9.96 us -> none  [on_device(): full_cot = lax.all_gather(cotangent, 'narrow', axis=0, tiled=True)]
    gather x2 -> x1, local copies, waits for them, and re-layouts: 42.2 us -> 34.5 us  [on_device(): jnp.take(flat_fetched, flat_slot, axis=0)]
  transfers between devices with their start and end apart: 4 -> 2, of which waited for: 4 -> 2; matrix products, arithmetic and copies ran while one was open for 1% -> 1% of each run, Pallas kernels for 0% -> 0%
where the time goes in v1:
time: 348 us; the launch traced here: 347 us
  waiting for transfers between devices  146 us (42%)
  local copies, waits for them, and re-layouts  125 us (36%)
  Pallas kernels  40.4 us (12%)
  starting transfers between devices  18.7 us (5%)
  other arithmetic  15.9 us (5%)
    all_to_all x1, waiting for transfers between devices, on_device(): lax.all_to_all(found, 'wide', split_axis=0, concat_axis=0, tiled=True)  140 us
    gather x1, local copies, waits for them, and re-layouts, on_device(): jnp.take(table, lax.all_to_all(buffer, 'wide', split_axis=0, concat_axis=...  48.5 us
    pallas_call x1, Pallas kernels, tail(): pl.pallas_call(tail_kernel, out_shape=(jax.ShapeDtypeStruct((128, 256), j...  40.4 us
    gather x1, local copies, waits for them, and re-layouts, on_device(): jnp.take(flat_fetched, flat_slot, axis=0)  34.5 us
    scatter x1, local copies, waits for them, and re-layouts, on_device(): buffer = jnp.zeros((wide_count * capacity,), jnp.int32).at[flat_slot].set...  30.5 us
    all_to_all x1, starting transfers between devices, on_device(): lax.all_to_all(buffer, 'wide', split_axis=0, concat_axis=0, tiled=True)  13.1 us
    unnamed x14, local copies, waits for them, and re-layouts  9.87 us
    select_n x2, other arithmetic, on_device(): jnp.take(table, lax.all_to_all(buffer, 'wide', split_axis=0, concat_axis=...  7.84 us
  transfers between devices with their start and end apart: 2, of which 2 were waited for; matrix products, arithmetic and copies ran while one was open for 1% of the time, Pallas kernels for 0%

profile of v1, /device:TPU:1, one launch (start us, length us, event | category | flops | bytes accessed | tf_op | source)
XLA Modules:
  0.0 347.5 jit_solution(8179043677025745588)
XLA Ops:
  0.6 0.0 copy-start.3
  0.6 0.0 copy-start
  0.6 1.0 copy.23
  1.7 0.8 copy_multiply_fusion
  2.5 0.1 eq.17
  2.6 0.6 convert_reduce_fusion.1
  3.2 0.1 reduce_window_sum.11
  3.3 0.8 fusion
  4.2 0.1 copy.25
  4.3 0.2 mul.29
  4.5 0.0 copy-done.3
  4.5 0.1 copy.26
  4.6 0.1 reshape.155
  4.7 0.1 compare_select_fusion.1
  4.8 30.5 %scatter_custom_fusion = s32[12288]{0:T(1024)S(1)} fusion(s32[8192]{0:T(1024)S(1)} %bitcast.35, s32[8192]{0:T(1024)S(1)} %reshape.155, s32[]{:T(128)} %constant.25.clone.1), kind=kCustom, calls=%fused_computation.28 | custom fusion | bytes 49156 | tf_op jit(solution)/shard_map/scatter | solution.py:182
  35.3 0.8 all_to_all.13
  36.0 13.1 %all-to-all-start = ((s32[64,1,192]{2,1,0:T(1,128)}), s32[64,1,192]{2,1,0:T(1,128)S(1)}, u32[]{:S(2)}, u32[]{:S(2)}) async-start(s32[64,1,192]{2,1,0:T(1,128)} %all_to_all.13), calls=%async_computation | async-start | bytes 131072 | tf_op jit(solution)/shard_map/all_to_all | solution.py:187
  49.2 0.0 copy-done
  49.2 4.0 %copy.27 = bf16[192,8192]{0,1:T(8,128)(2,1)} copy(bf16[192,8192]{1,0:T(8,128)(2,1)S(1)} %copy-done) | data formatting | bytes 6291456 | tf_op args[0]
  53.2 5.8 %all-to-all-done = s32[64,1,192]{2,1,0:T(1,128)S(1)} async-done(((s32[64,1,192]{2,1,0:T(1,128)}), s32[64,1,192]{2,1,0:T(1,128)S(1)}, u32[]{:S(2)}, u32[]{:S(2)}) %all-to-all-start) | async-done | bytes 49184 | tf_op jit(solution)/shard_map/all_to_all | solution.py:187
  59.0 0.2 fusion.3
  59.2 0.1 reshape.137
  59.3 48.5 %gather_fusion = bf16[12288,192]{1,0:T(8,128)(2,1)} fusion(bf16[8192,192]{1,0:T(8,128)(2,1)} %bitcast.31, s32[12288]{0:T(1024)S(1)} %broadcast_clamp_fusion), kind=kCustom, calls=%fused_computation | custom fusion | bytes 9486336 | tf_op jit(solution)/shard_map/jit(_take)/gather | solution.py:186
  107.9 7.6 %broadcast_select_fusion = bf16[64,192,192]{2,1,0:T(8,128)(2,1)} fusion(bf16[64,192,192]{2,1,0:T(8,128)(2,1)} %bitcast.32, pred[64,192]{1,0:T(8,128)(4,1)S(1)} %compare_and_fusion), kind=kLoop, calls=%fused_computation.4 | loop fusion | flops 2359296 | bytes 9449472 | tf_op jit(solution)/shard_map/jit(_take)/select_n | solution.py:186
  115.5 0.0 slice-start
  115.5 0.0 slice-start.1
  115.5 0.0 copy-start.2
  115.5 0.0 copy-start.1
  115.5 5.6 %all-to-all-start.1 = ((bf16[64,192,192]{2,1,0:T(8,128)(2,1)}), bf16[64,192,192]{2,1,0:T(8,128)(2,1)}, u32[]{:S(2)}, u32[]{:S(2)}) async-start(bf16[64,192,192]{2,1,0:T(8,128)(2,1)} %broadcast_select_fusion), calls=%async_computation.1 | async-start | bytes 12582912 | tf_op jit(solution)/shard_map/all_to_all | solution.py:189
  121.1 0.1 convert_element_type.32
  121.2 0.1 copy.24
  121.3 0.0 slice-done
  121.3 0.0 slice-done.1
  121.3 0.0 copy-done.2
  121.3 0.7 pad_maximum_fusion.1.w_ref
  122.0 0.0 copy-done.1
  122.1 139.9 %all-to-all-done.1 = bf16[64,192,192]{2,1,0:T(8,128)(2,1)} async-done(((bf16[64,192,192]{2,1,0:T(8,128)(2,1)}), bf16[64,192,192]{2,1,0:T(8,128)(2,1)}, u32[]{:S(2)}, u32[]{:S(2)}) %all-to-all-start.1) | async-done | bytes 4718624 | tf_op jit(solution)/shard_map/all_to_all | solution.py:189
  262.0 34.5 %gather_fusion.1 = bf16[8192,192]{1,0:T(8,128)(2,1)} fusion(bf16[12288,192]{1,0:T(8,128)(2,1)} %bitcast.8, s32[8192]{0:T(1024)S(1)} %broadcast_clamp_fusion.1), kind=kCustom, calls=%fused_computation.1 | custom fusion | bytes 6324224 | tf_op jit(solution)/shard_map/jit(_take)/gather | solution.py:191
  296.4 4.2 %copy_select_fusion = bf16[512,16,192]{2,0,1:T(8,128)(2,1)S(1)} fusion(bf16[512,16,192]{2,1,0:T(8,128)(2,1)} %bitcast.33, pred[512,16]{0,1:T(8,128)(4,1)S(1)} %compare_and_fusion.1), kind=kLoop, calls=%fused_computation.5 | loop fusion | flops 1572864 | bytes 6299648 | tf_op jit(solution)/shard_map/jit(_take)/select_n | solution.py:191
  300.6 0.7 convert_reduce_fusion
  301.4 0.9 pad_maximum_fusion.rows_ref
  302.3 40.4 %tail.1 = (bf16[128,256]{1,0:T(8,128)(2,1)}, f32[192,256]{1,0:T(8,128)}, f32[192,256]{1,0:T(8,128)}) custom-call(bf16[512,384]{1,0:T(8,128)(2,1)} %pad_maximum_fusion.rows_ref, bf16[384,256]{1,0:T(8,128)(2,1)} %pad_maximum_fusion.1.w_ref, bf16[128,256]{1,0:T(8,128)(2,1)} %cot_ref.1), custom_call_target="tpu_custom_call" | custom-call | tf_op jit(solution)/shard_map/tail/pallas_call | solution.py:125
  342.8 1.5 copy.40
  344.3 1.6 copy.41
  345.9 1.6 copy.42
  (10 shorter events, 0.2 us)
Async XLA Ops:
  0.6 3.8 %copy-start.3 = (s32[512,16]{0,1:T(8,128)S(1)}, s32[512,16]{0,1:T(8,128)}, u32[]{:S(2)}) copy-start(s32[512,16]{0,1:T(8,128)} %param.8) | copy-start | bytes 98308
  0.6 48.6 %copy-start = (bf16[192,8192]{1,0:T(8,128)(2,1)S(1)}, bf16[192,8192]{1,0:T(8,128)(2,1)}, u32[]{:S(2)}) copy-start(bf16[192,8192]{1,0:T(8,128)(2,1)} %param.6) | copy-start | bytes 9437188
  36.0 22.9 %all-to-all-start = ((s32[64,1,192]{2,1,0:T(1,128)}), s32[64,1,192]{2,1,0:T(1,128)S(1)}, u32[]{:S(2)}, u32[]{:S(2)}) async-start(s32[64,1,192]{2,1,0:T(1,128)} %all_to_all.13), calls=%async_computation | async-start | bytes 131072 | tf_op jit(solution)/shard_map/all_to_all | solution.py:187
  115.5 5.8 %slice-start = ((bf16[192,256]{1,0:T(8,128)(2,1)}), bf16[128,256]{1,0:T(8,128)(2,1)S(1)}, s32[]{:S(2)}) async-start(bf16[192,256]{1,0:T(8,128)(2,1)} %param.10), calls=%async_computation.2 | async-start | bytes 131072 | tf_op jit(solution)/shard_map/slice | solution.py:195
  115.5 5.8 %slice-start.1 = ((bf16[192,256]{1,0:T(8,128)(2,1)}), bf16[64,256]{1,0:T(8,128)(2,1)S(1)}, s32[]{:S(2)}) async-start(bf16[192,256]{1,0:T(8,128)(2,1)} %param.10), calls=%async_computation.3 | async-start | bytes 65536 | tf_op jit(solution)/shard_map/slice | solution.py:195
  115.5 5.8 %copy-start.2 = (bf16[192,256]{1,0:T(8,128)(2,1)S(1)}, bf16[192,256]{1,0:T(8,128)(2,1)}, u32[]{:S(2)}) copy-start(bf16[192,256]{1,0:T(8,128)(2,1)} %param.9) | copy-start | bytes 294916
  115.5 6.6 %copy-start.1 = (s32[512,16,1]{0,2,1:T(1,128)S(1)}, s32[512,16,1]{0,2,1:T(1,128)}, u32[]{:S(2)}) copy-start(s32[512,16,1]{0,2,1:T(1,128)} %param.7) | copy-start | bytes 98308
  115.5 146.5 %all-to-all-start.1 = ((bf16[64,192,192]{2,1,0:T(8,128)(2,1)}), bf16[64,192,192]{2,1,0:T(8,128)(2,1)}, u32[]{:S(2)}, u32[]{:S(2)}) async-start(bf16[64,192,192]{2,1,0:T(8,128)(2,1)} %broadcast_select_fusion), calls=%async_computation.1 | async-start | bytes 12582912 | tf_op jit(solution)/shard_map/all_to_all | solution.py:189

commit v2 on v1

--- a/solution.py
+++ b/solution.py
@@ -150,48 +150,277 @@
     )(rows, weights, cotangent)
 
 
-def slot_numbers(owners, wide_count, total):
-    block_rows = 128
-    block_count = total // block_rows
-    onehot = (owners[:, None] == jnp.arange(wide_count, dtype=jnp.int32)[None, :]).astype(
-        jnp.float32
+def order_of(step):
+    odd = lax.rem(step, 2)
+    return jnp.where(step == 0, 4, jnp.where(odd == 1, 3 - step // 2, 4 + step // 2))
+
+
+def list_requests(own_ref, row_ref, listed):
+    upper = (
+        lax.broadcasted_iota(jnp.int32, (512, 512), 0) < lax.broadcasted_iota(jnp.int32, (512, 512), 1)
+    ).astype(jnp.float32).astype(jnp.bfloat16)
+    owner_id = lax.broadcasted_iota(jnp.int32, (64, 512), 0)
+    slot_id = lax.broadcasted_iota(jnp.int32, (256, 512), 0)
+    slot_id = jnp.where(slot_id < 192, slot_id, slot_id - 64)
+    lane = lax.broadcasted_iota(jnp.int32, (1, 512), 1)
+
+    def one(j, carry):
+        used, found = carry
+        owner = own_ref[j]
+        row = row_ref[pl.ds(j, 1), :]
+        place_of = ((owner >> 1) & 7) * 8 + (owner >> 4) * 2 + (owner & 1)
+        mine = owner_id == place_of
+        onehot = jnp.where(mine, 1.0, 0.0)
+        within = jnp.dot(onehot.astype(jnp.bfloat16), upper, preferred_element_type=jnp.float32)
+        slot = jnp.sum(onehot * (within + used), axis=0, keepdims=True).astype(jnp.int32)
+        spot = jnp.where(slot_id == slot, 1.0, 0.0).astype(jnp.bfloat16)
+        pieces = [row & 255, row >> 8, lane & 255, (lane >> 8) + 2 * j + 1]
+        stacked = jnp.concatenate(
+            [jnp.where(mine, piece.astype(jnp.float32), 0.0) for piece in pieces], axis=0
+        ).astype(jnp.bfloat16)
+        found = found + lax.dot_general(
+            stacked, spot, (((1,), (1,)), ((), ())), preferred_element_type=jnp.float32
+        )
+        return used + jnp.sum(onehot, axis=1, keepdims=True), found
+
+    _, found = lax.fori_loop(
+        0, 16, one, (jnp.zeros((64, 1), jnp.float32), jnp.zeros((256, 256), jnp.float32))
     )
-    blocked = onehot.reshape(block_count, block_rows, wide_count)
-    lower = (jnp.arange(block_rows)[:, None] > jnp.arange(block_rows)[None, :]).astype(jnp.float32)
-    within = jnp.einsum("ij,bjw->biw", lower, blocked, precision=lax.Precision.HIGHEST)
-    block_sums = jnp.sum(blocked, axis=1)
-    offsets = jnp.cumsum(block_sums, axis=0) - block_sums
-    prefix = within + offsets[:, None, :]
-    return jnp.sum(prefix * blocked, axis=2).reshape(total).astype(jnp.int32)
+    found = found.astype(jnp.int32)
+    row = found[0:64] + 256 * found[64:128]
+    block = found[192:256]
+    item = found[128:192] + 256 * (block - 1)
+    target = jnp.where(block > 0, jnp.where(item < 512, item, 512 + (item & 511)), 1024)
+    listed[...] = (row + 8192 * target).reshape(8, 8, 256)
+
+
+def front_kernel(
+    feat_ref, own_ref, row_ref, out_ref,
+    listed, via, turned, asked, rows_of, index, dest, table, near, outgoing, landed, choose, held, dense, ring, ringed,
+    a_send, a_recv, b_send, b_recv, i_sem, f_send, f_recv, o_sem, r_send, r_recv,
+):
+    y, z, core, x = place()
+    near_z = [{"wide": wide_at(y, lax.rem(z + k, NZ), core), "narrow": x} for k in range(1, NZ)]
+
+    def plane(q):
+        return lax.rem(y + q // 2, NY), lax.rem(core + q, 2)
+
+    def plane_at(q):
+        there, seat = plane(q)
+        return {"wide": wide_at(there, z, seat), "narrow": x}
+
+    greet(near_z + [plane_at(q) for q in range(1, 8)])
+    me = y * 2 + core
+
+    list_requests(own_ref, row_ref, listed)
+    for k in range(1, NZ):
+        remote(listed.at[lax.rem(z + k, NZ)], via.at[z], a_send.at[k - 1], a_recv.at[k - 1], near_z[k - 1]).start()
+    via[z] = listed[z]
+
+    eye = (
+        lax.broadcasted_iota(jnp.int32, (256, 256), 0) == lax.broadcasted_iota(jnp.int32, (256, 256), 1)
+    ).astype(jnp.float32).astype(jnp.bfloat16)
+
+    def turn(b, _):
+        start = pl.multiple_of(b * 256, 256)
+        block = feat_ref[:, pl.ds(start, 256)]
+        block = jnp.concatenate([block, block[128:]], axis=0)
+        table[pl.ds(start, 256), :] = lax.dot_general(
+            eye, block, (((1,), (1,)), ((), ())), preferred_element_type=jnp.float32
+        )
+        return 0
+
+    lax.fori_loop(0, 16, turn, 0)
+    for k in range(1, NZ):
+        remote(listed.at[z], via.at[lax.rem(z + NZ - k, NZ)], a_send.at[k - 1], a_recv.at[k - 1], near_z[k - 1]).wait_recv()
+    for group in range(8):
+        for owner in range(8):
+            turned[owner, group:group + 1] = via[group, owner:owner + 1]
+
+    def tell(q, _):
+        there, seat = plane(q)
+        remote(turned.at[there * 2 + seat], asked.at[me], b_send.at[q], b_recv.at[q], plane_at(q)).start()
+        return 0
+
+    lax.fori_loop(1, 8, tell, 0)
+    asked[me] = turned[me]
+    for owner in range(8):
+        dest[:, owner * 192:(owner + 1) * 192] = turned[owner][:, :192] >> 13
+    lax.fori_loop(16, 32, turn, 0)
+
+    def told(q, _):
+        remote(turned.at[0], asked.at[0], b_send.at[q], b_recv.at[q], plane_at(q)).wait_recv()
+        return 0
+
+    lax.fori_loop(1, 8, told, 0)
+    rows_of[...] = (asked[...] & 8191).reshape(64, 256)
+    copy = pltpu.make_async_copy(rows_of, index, i_sem)
+    copy.start()
+    copy.wait()
+
+    low_half = lax.broadcasted_iota(jnp.int32, (96, 128), 1) < 64
+    low_lane = lax.broadcasted_iota(jnp.int32, (512, 128), 1) < 64
+
+    def fetch(step):
+        group = lax.rem(z + order_of(step), NZ)
+
+        def one(q, _):
+            there, seat = plane(q)
+            line = (there * 2 + seat) * 8 + group
+
+            def pick(s, _):
+                for u in range(8):
+                    node = index[line, s * 8 + u]
+                    near[s, u:u + 1, :] = table[pl.ds(node, 1), :]
+                return 0
+
+            lax.fori_loop(0, 24, pick, 0)
+            wide_rows = near[...].reshape(192, 256)
+            outgoing[step, q, 0:192] = wide_rows[:, :128].astype(jnp.bfloat16)
+            outgoing[step, q, 192:288] = jnp.where(low_half, wide_rows[:96, 128:], wide_rows[96:, 128:]).astype(jnp.bfloat16)
+
+            @pl.when(q > 0)
+            def _():
+                remote(outgoing.at[step, q], landed.at[step, me], f_send.at[step, q], f_recv.at[step, q], plane_at(q)).start()
+
+            @pl.when(q == 0)
+            def _():
+                pltpu.make_async_copy(outgoing.at[step, q], landed.at[step, me], o_sem.at[step]).start()
+
+            return 0
+
+        lax.fori_loop(0, 8, one, 0)
+
+    def gather_in(step):
+        group = lax.rem(z + order_of(step), NZ)
+        target_id = lax.broadcasted_iota(jnp.int32, (1024, 256), 0)
+        for b in range(6):
+            choose[:, b * 256:(b + 1) * 256] = jnp.where(
+                target_id == dest[pl.ds(group, 1), b * 256:(b + 1) * 256], 1.0, 0.0
+            ).astype(jnp.bfloat16)
+        pltpu.make_async_copy(outgoing.at[step, 0], landed.at[step, me], o_sem.at[step]).wait()
+
+        def got(q, _):
+            remote(outgoing.at[step, q], landed.at[step, me], f_send.at[step, q], f_recv.at[step, q], plane_at(q)).wait_recv()
+            return 0
+
+        lax.fori_loop(1, 8, got, 0)
+        for owner in range(8):
+            base = owner * 192
+            held[base:base + 192, 0:128] = landed[step, owner, 0:192]
+            pair = landed[step, owner, 192:288]
+            held[base:base + 96, 128:256] = pair
+            held[base + 96:base + 192, 128:256] = pltpu.roll(pair.astype(jnp.float32), 64, 1).astype(jnp.bfloat16)
+        for part in range(4):
+            dense[part * 256:(part + 1) * 256] = jnp.dot(
+                choose[part * 256:(part + 1) * 256], held[...], preferred_element_type=jnp.float32
+            )
+
+    def pieces():
+        mixed = jnp.where(low_lane, dense[0:512, 128:256], pltpu.roll(dense[512:1024, 128:256], 64, 1))
+        return [dense[0:512, 0:128], mixed, dense[512:1024, 0:128]]
+
+    def ring_at(step):
+        up = jnp.logical_or(step == 0, lax.rem(step, 2) == 1)
+        return {"wide": wide_at(y, lax.rem(z + jnp.where(up, 1, NZ - 1), NZ), core), "narrow": x}
+
+    def ring_copy(step):
+        return remote(ring.at[step], ringed.at[step], r_send.at[step], r_recv.at[step], ring_at(step))
+
+    def pass_on(step):
+        @pl.when(jnp.logical_or(step == 0, step == 2))
+        def _():
+            for i, piece in enumerate(pieces()):
+                ring[step, i] = piece.astype(jnp.bfloat16)
+
+        @pl.when(jnp.logical_and(step != 0, step != 2))
+        def _():
+            before = jnp.where(step == 1, 0, step - 2)
+            ring_copy(before).wait_recv()
+            for i, piece in enumerate(pieces()):
+                ring[step, i] = (piece + ringed[before, i].astype(jnp.float32)).astype(jnp.bfloat16)
+
+        ring_copy(step).start()
+
+    fetch(0)
+
+    def loop(step, _):
+        fetch(step + 1)
+        gather_in(step)
+        pass_on(step)
+        return 0
+
+    lax.fori_loop(0, 7, loop, 0)
+    gather_in(7)
+    ring_copy(5).wait_recv()
+    ring_copy(6).wait_recv()
+    for i, piece in enumerate(pieces()):
+        total = piece + ringed[5, i].astype(jnp.float32) + ringed[6, i].astype(jnp.float32)
+        if i == 1:
+            total = jnp.where(low_lane, total, total / FANOUT)
+        if i == 2:
+            total = total / FANOUT
+        out_ref[:, i * 128:(i + 1) * 128] = total.astype(jnp.bfloat16)
+
+    for k in range(1, NZ):
+        remote(listed.at[z], via.at[z], a_send.at[k - 1], a_recv.at[k - 1], near_z[k - 1]).wait_send()
+
+    def drain(q, _):
+        remote(turned.at[0], asked.at[0], b_send.at[q], b_recv.at[q], plane_at(q)).wait_send()
+
+        def each(step, _):
+            remote(outgoing.at[step, q], landed.at[step, me], f_send.at[step, q], f_recv.at[step, q], plane_at(q)).wait_send()
+            return 0
+
+        lax.fori_loop(0, 8, each, 0)
+        return 0
+
+    lax.fori_loop(1, 8, drain, 0)
+
+    def drain_ring(step, _):
+        ring_copy(step).wait_send()
+        return 0
+
+    lax.fori_loop(0, 7, drain_ring, 0)
+
+
+def front(features, owner_of, row_of):
+    vmem = pl.BlockSpec(memory_space=pltpu.VMEM)
+    dma = pltpu.SemaphoreType.DMA
+    return pl.pallas_call(
+        front_kernel,
+        out_shape=jax.ShapeDtypeStruct((512, 384), jnp.bfloat16),
+        in_specs=[vmem] * 3,
+        out_specs=vmem,
+        scratch_shapes=[
+            pltpu.VMEM((8, 8, 256), jnp.int32),
+            pltpu.VMEM((8, 8, 256), jnp.int32),
+            pltpu.VMEM((8, 8, 256), jnp.int32),
+            pltpu.VMEM((8, 8, 256), jnp.int32),
+            pltpu.VMEM((64, 256), jnp.int32),
+            pltpu.SMEM((64, 256), jnp.int32),
+            pltpu.VMEM((8, 1536), jnp.int32),
+            pltpu.VMEM((8192, 256), jnp.float32),
+            pltpu.VMEM((24, 8, 256), jnp.float32),
+            pltpu.VMEM((8, 8, 288, 128), jnp.bfloat16),
+            pltpu.VMEM((8, 8, 288, 128), jnp.bfloat16),
+            pltpu.VMEM((1024, 1536), jnp.bfloat16),
+            pltpu.VMEM((1536, 256), jnp.bfloat16),
+            pltpu.VMEM((1024, 256), jnp.float32),
+            pltpu.VMEM((7, 3, 512, 128), jnp.bfloat16),
+            pltpu.VMEM((7, 3, 512, 128), jnp.bfloat16),
+            dma((NZ - 1,)), dma((NZ - 1,)), dma((8,)), dma((8,)), dma(()),
+            dma((8, 8)), dma((8, 8)), dma((8,)), dma((7,)), dma((7,)),
+        ],
+        compiler_params=pltpu.CompilerParams(
+            collective_id=1, has_side_effects=True, vmem_limit_bytes=60 * 1024 * 1024
+        ),
+        name="front",
+    )(features, jnp.transpose(owner_of, (1, 2, 0)), jnp.transpose(row_of))
 
 
 def on_device(features, owner_of, row_of, w_self, w_neighbor, cotangent):
-    wide_count = lax.axis_size("wide")
-    narrow_count = lax.axis_size("narrow")
-    tgt_rows, request_count = row_of.shape
-    feat_cols = features.shape[0]
-    total = tgt_rows * request_count
-    capacity = max(2, 3 * total // (2 * wide_count))
-    owners = owner_of.reshape(total)
-    wanted = row_of.reshape(total)
-    slot_of = slot_numbers(owners, wide_count, total)
-    flat_slot = owners * capacity + slot_of
-    buffer = (
-        jnp.zeros((wide_count * capacity,), jnp.int32)
-        .at[flat_slot]
-        .set(wanted)
-        .reshape(wide_count, capacity)
-    )
-    table = jnp.transpose(features)
-    found = jnp.take(
-        table, lax.all_to_all(buffer, "wide", split_axis=0, concat_axis=0, tiled=True), axis=0
-    )
-    fetched = lax.all_to_all(found, "wide", split_axis=0, concat_axis=0, tiled=True)
-    flat_fetched = fetched.reshape(wide_count * capacity, feat_cols)
-    gathered = jnp.take(flat_fetched, flat_slot, axis=0).reshape(tgt_rows, request_count, feat_cols)
-    self_rows = gathered[:, 0]
-    pooled = (jnp.sum(gathered[:, 1:], axis=1, dtype=jnp.float32) / FANOUT).astype(jnp.bfloat16)
-    rows = jnp.concatenate([self_rows, pooled[:, 128:], pooled[:, :128]], axis=1)
+    rows = front(features, owner_of, row_of)
     weights = jnp.concatenate([w_self, w_neighbor[128:], w_neighbor[:128]], axis=0)
     return tail(rows, weights, cotangent)
 

time: 348 us -> 160 us (0.46)
  waiting for transfers between devices: 146 us -> 0 us
  local copies, waits for them, and re-layouts: 125 us -> 6.31 us
  Pallas kernels: 40.4 us -> 151 us
  starting transfers between devices: 18.7 us -> 0 us
  other arithmetic: 15.9 us -> 1.58 us
    all_to_all x2 -> x0, waiting for transfers between devices: 146 us -> none  [the longest x1 140 us: on_device(): lax.all_to_all(found, 'wide', split_axis=0, concat_axis=0, tiled=True)]
    pallas_call x0 -> x1, Pallas kernels: none -> 111 us  [front(): pl.pallas_call(front_kernel, out_shape=jax.ShapeDtypeStruct((512, 384), j...]
    gather x2 -> x0, local copies, waits for them, and re-layouts: 83 us -> none  [the longest x1 48.5 us: on_device(): jnp.take(table, lax.all_to_all(buffer, 'wide', split_axis=0, concat_axis=...]
    scatter x1 -> x0, local copies, waits for them, and re-layouts: 30.5 us -> none  [on_device(): buffer = jnp.zeros((wide_count * capacity,), jnp.int32).at[flat_slot].set...]
    all_to_all x2 -> x0, starting transfers between devices: 18.7 us -> none  [the longest x1 13.1 us: on_device(): lax.all_to_all(buffer, 'wide', split_axis=0, concat_axis=0, tiled=True)]
    select_n x4 -> x0, other arithmetic: 12.1 us -> none  [the longest x2 7.84 us: on_device(): jnp.take(table, lax.all_to_all(buffer, 'wide', split_axis=0, concat_axis=...]
    unnamed x14 -> x3, local copies, waits for them, and re-layouts: 9.87 us -> 4.7 us
  transfers between devices with their start and end apart: 2 -> 0, of which waited for: 2 -> 0; matrix products, arithmetic and copies ran while one was open for 1% -> 0% of each run, Pallas kernels for 0% -> 0%
where the time goes in v2:
time: 160 us
  Pallas kernels  151 us (94%)
  local copies, waits for them, and re-layouts  6.31 us (4%)
    pallas_call x1, Pallas kernels, front(): pl.pallas_call(front_kernel, out_shape=jax.ShapeDtypeStruct((512, 384), j...  111 us
    pallas_call x1, Pallas kernels, tail(): pl.pallas_call(tail_kernel, out_shape=(jax.ShapeDtypeStruct((128, 256), j...  40.8 us
    unnamed x3, local copies, waits for them, and re-layouts  4.7 us

profile of v2, /device:TPU:1, one launch (start us, length us, event | category | flops | bytes accessed | tf_op | source)
XLA Modules:
  0.0 159.8 jit_solution(9211524812370033302)
XLA Ops:
  0.6 0.8 slice.6
  1.4 0.8 slice.7
  2.2 1.6 pad_maximum_fusion.w_ref
  3.8 110.5 %front.1.rows_ref = bf16[512,384]{1,0:T(8,128)(2,1)} custom-call(bf16[192,8192]{1,0:T(8,128)(2,1)} %feat_ref.1, s32[16,1,512]{2,1,0:T(1,128)} %bitcast.2, s32[16,512]{1,0:T(8,128)} %bitcast.3), custom_call_target="tpu_custom_call" | custom-call | tf_op jit(solution)/shard_map/front/pallas_call | solution.py:390
  114.3 40.8 %tail.1 = (bf16[128,256]{1,0:T(8,128)(2,1)}, f32[192,256]{1,0:T(8,128)}, f32[192,256]{1,0:T(8,128)}) custom-call(bf16[512,384]{1,0:T(8,128)(2,1)} %front.1.rows_ref, bf16[384,256]{1,0:T(8,128)(2,1)} %pad_maximum_fusion.w_ref, bf16[128,256]{1,0:T(8,128)(2,1)} %cot_ref.1), custom_call_target="tpu_custom_call" | custom-call | tf_op jit(solution)/shard_map/tail/pallas_call | solution.py:125
  155.1 1.5 copy.12
  156.6 1.6 %copy.13 = f32[192,256]{1,0:T(8,128)} copy(f32[192,256]{1,0:T(8,128)} %get-tuple-element.7) | data formatting | bytes 393216
  158.2 1.6 %copy.14 = f32[192,256]{1,0:T(8,128)} copy(f32[192,256]{1,0:T(8,128)} %get-tuple-element.8) | data formatting | bytes 393216

commit v3 on v2

v3 whole, which is shorter than its diff:
```python
import jax
import jax.numpy as jnp
from jax import lax
from jax.experimental import pallas as pl
from jax.experimental.pallas import tpu as pltpu
from jax.sharding import PartitionSpec as P

FANOUT = 15
NX, NY, NZ = 4, 4, 8
ROOT, CUBE = 0.7978845608, 0.044715


def remote(src, dst, send, recv, target):
    return pltpu.make_async_remote_copy(
        src_ref=src,
        dst_ref=dst,
        send_sem=send,
        recv_sem=recv,
        device_id=target,
        device_id_type=pl.DeviceIdType.MESH,
    )


def place():
    wide = lax.axis_index("wide")
    return wide // 16, lax.rem(wide // 2, 8), lax.rem(wide, 2), lax.axis_index("narrow")


def wide_at(y, z, core):
    return (y * 8 + z) * 2 + core


def order_of(step):
    odd = lax.rem(step, 2)
    return jnp.where(step == 0, 4, jnp.where(odd == 1, 3 - step // 2, 4 + step // 2))


def list_requests(own_ref, row_ref, listed):
    upper = (
        lax.broadcasted_iota(jnp.int32, (512, 512), 0) < lax.broadcasted_iota(jnp.int32, (512, 512), 1)
    ).astype(jnp.float32).astype(jnp.bfloat16)
    owner_id = lax.broadcasted_iota(jnp.int32, (64, 512), 0)
    slot_id = lax.broadcasted_iota(jnp.int32, (256, 512), 0)
    slot_id = jnp.where(slot_id < 192, slot_id, slot_id - 64)
    lane = lax.broadcasted_iota(jnp.int32, (1, 512), 1)

    def one(j, carry):
        used, found = carry
        owner = own_ref[j]
        row = row_ref[pl.ds(j, 1), :]
        place_of = ((owner >> 1) & 7) * 8 + (owner >> 4) * 2 + (owner & 1)
        mine = owner_id == place_of
        onehot = jnp.where(mine, 1.0, 0.0)
        within = jnp.dot(onehot.astype(jnp.bfloat16), upper, preferred_element_type=jnp.float32)
        slot = jnp.sum(onehot * (within + used), axis=0, keepdims=True).astype(jnp.int32)
        spot = jnp.where(slot_id == slot, 1.0, 0.0).astype(jnp.bfloat16)
        pieces = [row & 255, row >> 8, lane & 255, (lane >> 8) + 2 * j + 1]
        stacked = jnp.concatenate(
            [jnp.where(mine, piece.astype(jnp.float32), 0.0) for piece in pieces], axis=0
        ).astype(jnp.bfloat16)
        found = found + lax.dot_general(
            stacked, spot, (((1,), (1,)), ((), ())), preferred_element_type=jnp.float32
        )
        return used + jnp.sum(onehot, axis=1, keepdims=True), found

    _, found = lax.fori_loop(
        0, 16, one, (jnp.zeros((64, 1), jnp.float32), jnp.zeros((256, 256), jnp.float32))
    )
    found = found.astype(jnp.int32)
    row = found[0:64] + 256 * found[64:128]
    block = found[192:256]
    item = found[128:192] + 256 * (block - 1)
    target = jnp.where(block > 0, jnp.where(item < 512, item, 512 + (item & 511)), 1024)
    listed[...] = (row + 8192 * target).reshape(8, 8, 256)


def step_kernel(
    feat_ref, own_ref, row_ref, ws_ref, wn_ref, cot_ref, hid_ref, final,
    feat, listed, via, turned, asked, rows_of, index, dest, table, near, outgoing, landed, choose, held, dense, ring, ringed,
    rows, part, part_out, got_part, slopes, grads, got_core, full, full_out, got_z, got_y,
    e_sem, a_send, a_recv, b_send, b_recv, i_sem, f_send, f_recv, o_sem, r_send, r_recv,
    x_send, x_recv, s_send, s_recv, c_send, c_recv, z_send, z_recv, y_send, y_recv, g_send, g_recv, d_send, d_recv,
):
    y, z, core, x = place()
    near_z = [{"wide": wide_at(y, lax.rem(z + k, NZ), core), "narrow": x} for k in range(1, NZ)]
    near_x = [{"wide": wide_at(y, z, core), "narrow": lax.rem(x + k, NX)} for k in range(1, NX)]

    def plane(q):
        return lax.rem(y + q // 2, NY), lax.rem(core + q, 2)

    def plane_at(q):
        there, seat = plane(q)
        return {"wide": wide_at(there, z, seat), "narrow": x}

    barrier = pltpu.get_barrier_semaphore()
    targets = near_z + [plane_at(q) for q in range(1, 8)] + near_x
    for target in targets:
        pl.semaphore_signal(barrier, inc=1, device_id=target, device_id_type=pl.DeviceIdType.MESH)
    feat_copy = pltpu.make_async_copy(feat_ref, feat, e_sem)
    feat_copy.start()
    me = y * 2 + core

    list_requests(own_ref, row_ref, listed)
    pl.semaphore_wait(barrier, len(targets))
    for k in range(1, NZ):
        remote(listed.at[lax.rem(z + k, NZ)], via.at[z], a_send.at[k - 1], a_recv.at[k - 1], near_z[k - 1]).start()
    via[z] = listed[z]

    eye = (
        lax.broadcasted_iota(jnp.int32, (256, 256), 0) == lax.broadcasted_iota(jnp.int32, (256, 256), 1)
    ).astype(jnp.float32).astype(jnp.bfloat16)

    def turn(b, _):
        start = pl.multiple_of(b * 256, 256)
        block = feat[:, pl.ds(start, 256)]
        block = jnp.concatenate([block, block[128:]], axis=0)
        turned_block = lax.dot_general(eye, block, (((1,), (1,)), ((), ())), preferred_element_type=jnp.float32)
        table[pl.ds(2 * start, 256, stride=2), :] = turned_block[:, :128]
        table[pl.ds(2 * start + 1, 256, stride=2), :] = turned_block[:, 128:]
        return 0

    feat_copy.wait()
    lax.fori_loop(0, 16, turn, 0)
    for k in range(1, NZ):
        remote(listed.at[z], via.at[lax.rem(z + NZ - k, NZ)], a_send.at[k - 1], a_recv.at[k - 1], near_z[k - 1]).wait_recv()
    for group in range(8):
        for owner in range(8):
            turned[owner, group:group + 1] = via[group, owner:owner + 1]

    def tell(q, _):
        there, seat = plane(q)
        remote(turned.at[there * 2 + seat], asked.at[me], b_send.at[q], b_recv.at[q], plane_at(q)).start()
        return 0

    lax.fori_loop(1, 8, tell, 0)
    asked[me] = turned[me]
    for owner in range(8):
        dest[:, owner * 192:(owner + 1) * 192] = turned[owner][:, :192] >> 13
    lax.fori_loop(16, 32, turn, 0)

    def told(q, _):
        remote(turned.at[0], asked.at[0], b_send.at[q], b_recv.at[q], plane_at(q)).wait_recv()
        return 0

    lax.fori_loop(1, 8, told, 0)
    rows_of[...] = 2 * (asked[...] & 8191).reshape(64, 256)
    copy = pltpu.make_async_copy(rows_of, index, i_sem)
    copy.start()
    copy.wait()

    low_half = lax.broadcasted_iota(jnp.int32, (96, 128), 1) < 64
    low_lane = lax.broadcasted_iota(jnp.int32, (512, 128), 1) < 64

    def fetch(step):
        group = lax.rem(z + order_of(step), NZ)

        def one(q, _):
            there, seat = plane(q)
            line = (there * 2 + seat) * 8 + group

            for s in range(192):
                near[2 * s:2 * s + 2, :] = table[pl.ds(index[line, s], 2), :]
            outgoing[step, q, 0:192] = near[pl.ds(0, 192, stride=2), :].astype(jnp.bfloat16)
            outgoing[step, q, 192:288] = jnp.where(
                low_half, near[pl.ds(1, 96, stride=2), :], near[pl.ds(193, 96, stride=2), :]
            ).astype(jnp.bfloat16)

            @pl.when(q > 0)
            def _():
                remote(outgoing.at[step, q], landed.at[step, me], f_send.at[step, q], f_recv.at[step, q], plane_at(q)).start()

            @pl.when(q == 0)
            def _():
                pltpu.make_async_copy(outgoing.at[step, q], landed.at[step, me], o_sem.at[step]).start()

            return 0

        lax.fori_loop(0, 8, one, 0)

    def gather_in(step):
        group = lax.rem(z + order_of(step), NZ)
        target_id = lax.broadcasted_iota(jnp.int32, (1024, 256), 0)
        for b in range(6):
            choose[:, b * 256:(b + 1) * 256] = jnp.where(
                target_id == dest[pl.ds(group, 1), b * 256:(b + 1) * 256], 1.0, 0.0
            ).astype(jnp.bfloat16)
        pltpu.make_async_copy(outgoing.at[step, 0], landed.at[step, me], o_sem.at[step]).wait()

        def got(q, _):
            remote(outgoing.at[step, q], landed.at[step, me], f_send.at[step, q], f_recv.at[step, q], plane_at(q)).wait_recv()
            return 0

        lax.fori_loop(1, 8, got, 0)
        for owner in range(8):
            base = owner * 192
            held[base:base + 192, 0:128] = landed[step, owner, 0:192]
            pair = landed[step, owner, 192:288]
            held[base:base + 96, 128:256] = pair
            held[base + 96:base + 192, 128:256] = pltpu.roll(pair.astype(jnp.float32), 64, 1).astype(jnp.bfloat16)
        for part in range(4):
            dense[part * 256:(part + 1) * 256] = jnp.dot(
                choose[part * 256:(part + 1) * 256], held[...], preferred_element_type=jnp.float32
            )

    def pieces():
        mixed = jnp.where(low_lane, dense[0:512, 128:256], pltpu.roll(dense[512:1024, 128:256], 64, 1))
        return [dense[0:512, 0:128], mixed, dense[512:1024, 0:128]]

    def ring_at(step):
        up = jnp.logical_or(step == 0, lax.rem(step, 2) == 1)
        return {"wide": wide_at(y, lax.rem(z + jnp.where(up, 1, NZ - 1), NZ), core), "narrow": x}

    def ring_copy(step):
        return remote(ring.at[step], ringed.at[step], r_send.at[step], r_recv.at[step], ring_at(step))

    def pass_on(step):
        @pl.when(jnp.logical_or(step == 0, step == 2))
        def _():
            for i, piece in enumerate(pieces()):
                ring[step, i] = piece.astype(jnp.bfloat16)

        @pl.when(jnp.logical_and(step != 0, step != 2))
        def _():
            before = jnp.where(step == 1, 0, step - 2)
            ring_copy(before).wait_recv()
            for i, piece in enumerate(pieces()):
                ring[step, i] = (piece + ringed[before, i].astype(jnp.float32)).astype(jnp.bfloat16)

        ring_copy(step).start()

    fetch(0)

    def loop(step, _):
        fetch(step + 1)
        gather_in(step)
        pass_on(step)
        return 0

    lax.fori_loop(0, 7, loop, 0)
    gather_in(7)
    ring_copy(5).wait_recv()
    ring_copy(6).wait_recv()
    for i, piece in enumerate(pieces()):
        total = piece + ringed[5, i].astype(jnp.float32) + ringed[6, i].astype(jnp.float32)
        if i == 1:
            total = jnp.where(low_lane, total, total / FANOUT)
        if i == 2:
            total = total / FANOUT
        rows[:, i * 128:(i + 1) * 128] = total.astype(jnp.bfloat16)

    middle = jnp.concatenate([ws_ref[128:192], wn_ref[128:192]], axis=0)
    for k in range(NX):
        span = slice(k * 128, (k + 1) * 128)
        value = jnp.dot(rows[span, 0:128], ws_ref[0:128], preferred_element_type=jnp.float32)
        value = value + jnp.dot(rows[span, 128:256], middle, preferred_element_type=jnp.float32)
        value = value + jnp.dot(rows[span, 256:384], wn_ref[0:128], preferred_element_type=jnp.float32)
        part[k] = value
        part_out[k] = value.astype(jnp.bfloat16)
    sent = []
    for k in range(1, NX):
        copy = remote(part_out.at[lax.rem(x + k, NX)], got_part.at[k - 1], x_send.at[k - 1], x_recv.at[k - 1], near_x[k - 1])
        copy.start()
        sent.append(copy)
    value = part[x]
    for k in range(1, NX):
        sent[k - 1].wait_recv()
        value = value + got_part[k - 1].astype(jnp.float32)
    bend = jnp.tanh(ROOT * (value + CUBE * value * value * value))
    rise = 0.5 * (1.0 + bend) + 0.5 * value * (1.0 - bend * bend) * ROOT * (1.0 + 3.0 * CUBE * value * value)
    slopes[x] = (cot_ref[...].astype(jnp.float32) * rise).astype(jnp.bfloat16)
    for k in range(1, NX):
        copy = remote(slopes.at[x], slopes.at[x], s_send.at[k - 1], s_recv.at[k - 1], near_x[k - 1])
        copy.start()
        sent.append(copy)
    hid_ref[...] = (0.5 * value * (1.0 + bend)).astype(jnp.bfloat16)
    for k in range(1, NX):
        remote(slopes.at[x], slopes.at[lax.rem(x + NX - k, NX)], s_send.at[k - 1], s_recv.at[k - 1], near_x[k - 1]).wait_recv()
    grads[...] = lax.dot_general(
        rows[...], slopes[...].reshape(512, 256), (((0,), (0,)), ((), ())), preferred_element_type=jnp.float32
    ).reshape(2, NZ, 24, 256)
    copy = remote(grads.at[1 - core], got_core, c_send, c_recv, plane_at(1))
    copy.start()
    sent.append(copy)
    copy.wait_recv()
    full[...] = grads[core] + got_core[...]
    full_out[...] = full[...].astype(jnp.bfloat16)
    for k in range(1, NZ):
        copy = remote(full_out.at[lax.rem(z + k, NZ)], got_z.at[k - 1], z_send.at[k - 1], z_recv.at[k - 1], near_z[k - 1])
        copy.start()
        sent.append(copy)
    mine = full[z]
    for k in range(1, NZ):
        remote(full_out.at[z], got_z.at[k - 1], z_send.at[k - 1], z_recv.at[k - 1], near_z[k - 1]).wait_recv()
        mine = mine + got_z[k - 1].astype(jnp.float32)
    got_y[y] = mine
    for k in range(1, NY):
        copy = remote(got_y.at[y], got_y.at[y], y_send.at[k - 1], y_recv.at[k - 1], plane_at(2 * k))
        copy.start()
        sent.append(copy)
    for k in range(1, NY):
        remote(got_y.at[y], got_y.at[lax.rem(y + NY - k, NY)], y_send.at[k - 1], y_recv.at[k - 1], plane_at(2 * k)).wait_recv()
    final[core, z] = (got_y[0] + got_y[1] + got_y[2] + got_y[3]).astype(jnp.bfloat16)
    for k in range(1, NZ):
        copy = remote(final.at[core, z], final.at[core, z], g_send.at[k - 1], g_recv.at[k - 1], near_z[k - 1])
        copy.start()
        sent.append(copy)
    for k in range(1, NZ):
        remote(final.at[core, z], final.at[core, lax.rem(z + NZ - k, NZ)], g_send.at[k - 1], g_recv.at[k - 1], near_z[k - 1]).wait_recv()
    copy = remote(final.at[core], final.at[core], d_send, d_recv, plane_at(1))
    copy.start()
    sent.append(copy)
    remote(final.at[core], final.at[1 - core], d_send, d_recv, plane_at(1)).wait_recv()
    for copy in sent:
        copy.wait_send()

    for k in range(1, NZ):
        remote(listed.at[z], via.at[z], a_send.at[k - 1], a_recv.at[k - 1], near_z[k - 1]).wait_send()

    def drain(q, _):
        remote(turned.at[0], asked.at[0], b_send.at[q], b_recv.at[q], plane_at(q)).wait_send()

        def each(step, _):
            remote(outgoing.at[step, q], landed.at[step, me], f_send.at[step, q], f_recv.at[step, q], plane_at(q)).wait_send()
            return 0

        lax.fori_loop(0, 8, each, 0)
        return 0

    lax.fori_loop(1, 8, drain, 0)

    def drain_ring(step, _):
        ring_copy(step).wait_send()
        return 0

    lax.fori_loop(0, 7, drain_ring, 0)


def finish_kernel(hid_ref, final_ref, out_ref, gs_ref, gn_ref):
    out_ref[...] = hid_ref[...]
    whole = final_ref[...].astype(jnp.float32).reshape(384, 256)
    gs_ref[...] = whole[:192]
    gn_ref[0:128] = whole[256:]
    gn_ref[128:192] = whole[192:256]


def on_device(features, owner_of, row_of, w_self, w_neighbor, cotangent):
    vmem = pl.BlockSpec(memory_space=pltpu.VMEM)
    dma = pltpu.SemaphoreType.DMA
    f32, bf16, i32 = jnp.float32, jnp.bfloat16, jnp.int32
    hidden, final = pl.pallas_call(
        step_kernel,
        out_shape=(jax.ShapeDtypeStruct((128, 256), bf16), jax.ShapeDtypeStruct((2, NZ, 24, 256), bf16)),
        in_specs=[pl.BlockSpec(memory_space=pl.ANY)] + [vmem] * 5,
        out_specs=(vmem, vmem),
        scratch_shapes=[
            pltpu.VMEM((192, 8192), bf16),
            pltpu.VMEM((8, 8, 256), i32),
            pltpu.VMEM((8, 8, 256), i32),
            pltpu.VMEM((8, 8, 256), i32),
            pltpu.VMEM((8, 8, 256), i32),
            pltpu.VMEM((64, 256), i32),
            pltpu.SMEM((64, 256), i32),
            pltpu.VMEM((8, 1536), i32),
            pltpu.VMEM((16384, 128), f32),
            pltpu.VMEM((384, 128), f32),
            pltpu.VMEM((8, 8, 288, 128), bf16),
            pltpu.VMEM((8, 8, 288, 128), bf16),
            pltpu.VMEM((1024, 1536), bf16),
            pltpu.VMEM((1536, 256), bf16),
            pltpu.VMEM((1024, 256), f32),
            pltpu.VMEM((7, 3, 512, 128), bf16),
            pltpu.VMEM((7, 3, 512, 128), bf16),
            pltpu.VMEM((512, 384), bf16),
            pltpu.VMEM((NX, 128, 256), f32),
            pltpu.VMEM((NX, 128, 256), bf16),
            pltpu.VMEM((NX - 1, 128, 256), bf16),
            pltpu.VMEM((NX, 128, 256), bf16),
            pltpu.VMEM((2, NZ, 24, 256), f32),
            pltpu.VMEM((NZ, 24, 256), f32),
            pltpu.VMEM((NZ, 24, 256), f32),
            pltpu.VMEM((NZ, 24, 256), bf16),
            pltpu.VMEM((NZ - 1, 24, 256), bf16),
            pltpu.VMEM((NY, 24, 256), f32),
            dma(()), dma((NZ - 1,)), dma((NZ - 1,)), dma((8,)), dma((8,)), dma(()),
            dma((8, 8)), dma((8, 8)), dma((8,)), dma((7,)), dma((7,)),
            dma((NX - 1,)), dma((NX - 1,)), dma((NX - 1,)), dma((NX - 1,)), dma(()), dma(()),
            dma((NZ - 1,)), dma((NZ - 1,)), dma((NY - 1,)), dma((NY - 1,)),
            dma((NZ - 1,)), dma((NZ - 1,)), dma(()), dma(()),
        ],
        compiler_params=pltpu.CompilerParams(
            collective_id=1, has_side_effects=True, vmem_limit_bytes=60 * 1024 * 1024
        ),
        name="step",
    )(features, jnp.transpose(owner_of, (1, 2, 0)), jnp.transpose(row_of), w_self, w_neighbor, cotangent)
    return pl.pallas_call(
        finish_kernel,
        out_shape=(
            jax.ShapeDtypeStruct((128, 256), bf16),
            jax.ShapeDtypeStruct((192, 256), f32),
            jax.ShapeDtypeStruct((192, 256), f32),
        ),
        in_specs=[vmem, vmem],
        out_specs=(vmem, vmem, vmem),
        name="finish",
    )(hidden, final)


def solution(mesh):
    return jax.shard_map(
        on_device,
        mesh=mesh,
        in_specs=(
            P("narrow", "wide"),
            P("wide", None, None),
            P("wide", None),
            P("narrow", None),
            P("narrow", None),
            P(("wide", "narrow"), None),
        ),
        out_specs=(P(("wide", "narrow"), None), P("narrow", None), P("narrow", None)),
        check_vma=False,
    )
```

time: 160 us -> 123 us (0.77)
  Pallas kernels: 151 us -> 123 us
  local copies, waits for them, and re-layouts: 6.31 us -> 0 us
    pallas_call x2, Pallas kernels: 151 us -> 123 us  [the longest x1 121 us: on_device(): pl.pallas_call(step_kernel, out_shape=(jax.ShapeDtypeStruct((128, 256), b...]
    unnamed x3 -> x0, local copies, waits for them, and re-layouts: 4.7 us -> none
    slice x2 -> x0, local copies, waits for them, and re-layouts: 1.61 us -> none  [the longest x1 0.84 us: on_device(): w_neighbor[:128]]
where the time goes in v3:
time: 123 us
  Pallas kernels  123 us (100%)
    pallas_call x1, Pallas kernels, on_device(): pl.pallas_call(step_kernel, out_shape=(jax.ShapeDtypeStruct((128, 256), b...  121 us

profile of v3, /device:TPU:1, one launch (start us, length us, event | category | flops | bytes accessed | tf_op | source)
XLA Modules:
  0.0 123.2 jit_solution(11649585808556111839)
XLA Ops:
  0.6 120.8 %step.1 = (bf16[128,256]{1,0:T(8,128)(2,1)}, bf16[2,8,24,256]{3,2,1,0:T(8,128)(2,1)}) custom-call(bf16[192,8192]{1,0:T(8,128)(2,1)} %feat_ref.1, s32[16,1,512]{2,1,0:T(1,128)} %bitcast.2, s32[16,512]{1,0:T(8,128)} %bitcast.3, bf16[192,256]{1,0:T(8,128)(2,1)} %ws_ref.1, bf16[192,256]{1,0:T(8,128)(2,1)} %wn_ref.1, bf16[128,256]{1,0:T(8,128)(2,1)} %cot_ref.1), custom_call_target="tpu_custom_call" | custom-call | tf_op jit(solution)/shard_map/step/pallas_call | solution.py:350
  121.5 1.7 %finish.1 = (bf16[128,256]{1,0:T(8,128)(2,1)}, f32[192,256]{1,0:T(8,128)}, f32[192,256]{1,0:T(8,128)}) custom-call(bf16[128,256]{1,0:T(8,128)(2,1)} %get-tuple-element.5.hid_ref, bf16[2,8,24,256]{3,2,1,0:T(8,128)(2,1)} %get-tuple-element.6.final_ref), custom_call_target="tpu_custom_call" | custom-call | tf_op jit(solution)/shard_map/finish/pallas_call | solution.py:395

commit v4 on v3

--- a/solution.py
+++ b/solution.py
@@ -35,7 +35,7 @@
     return jnp.where(step == 0, 4, jnp.where(odd == 1, 3 - step // 2, 4 + step // 2))
 
 
-def list_requests(own_ref, row_ref, listed):
+def list_requests(own_ref, row_ref, listed, stacked, spots):
     upper = (
         lax.broadcasted_iota(jnp.int32, (512, 512), 0) < lax.broadcasted_iota(jnp.int32, (512, 512), 1)
     ).astype(jnp.float32).astype(jnp.bfloat16)
@@ -44,8 +44,7 @@
     slot_id = jnp.where(slot_id < 192, slot_id, slot_id - 64)
     lane = lax.broadcasted_iota(jnp.int32, (1, 512), 1)
 
-    def one(j, carry):
-        used, found = carry
+    def one(j, used):
         owner = own_ref[j]
         row = row_ref[pl.ds(j, 1), :]
         place_of = ((owner >> 1) & 7) * 8 + (owner >> 4) * 2 + (owner & 1)
@@ -53,18 +52,15 @@
         onehot = jnp.where(mine, 1.0, 0.0)
         within = jnp.dot(onehot.astype(jnp.bfloat16), upper, preferred_element_type=jnp.float32)
         slot = jnp.sum(onehot * (within + used), axis=0, keepdims=True).astype(jnp.int32)
-        spot = jnp.where(slot_id == slot, 1.0, 0.0).astype(jnp.bfloat16)
-        pieces = [row & 255, row >> 8, lane & 255, (lane >> 8) + 2 * j + 1]
-        stacked = jnp.concatenate(
-            [jnp.where(mine, piece.astype(jnp.float32), 0.0) for piece in pieces], axis=0
-        ).astype(jnp.bfloat16)
-        found = found + lax.dot_general(
-            stacked, spot, (((1,), (1,)), ((), ())), preferred_element_type=jnp.float32
-        )
-        return used + jnp.sum(onehot, axis=1, keepdims=True), found
-
-    _, found = lax.fori_loop(
-        0, 16, one, (jnp.zeros((64, 1), jnp.float32), jnp.zeros((256, 256), jnp.float32))
+        span = pl.ds(pl.multiple_of(j * 512, 512), 512)
+        spots[:, span] = jnp.where(slot_id == slot, 1.0, 0.0).astype(jnp.bfloat16)
+        for i, piece in enumerate([row & 255, row >> 8, lane & 255, (lane >> 8) + 2 * j + 1]):
+            stacked[i * 64:(i + 1) * 64, span] = jnp.where(mine, piece.astype(jnp.float32), 0.0).astype(jnp.bfloat16)
+        return used + jnp.sum(onehot, axis=1, keepdims=True)
+
+    lax.fori_loop(0, 16, one, jnp.zeros((64, 1), jnp.float32))
+    found = lax.dot_general(
+        stacked[...], spots[...], (((1,), (1,)), ((), ())), preferred_element_type=jnp.float32
     )
     found = found.astype(jnp.int32)
     row = found[0:64] + 256 * found[64:128]
@@ -76,7 +72,7 @@
 
 def step_kernel(
     feat_ref, own_ref, row_ref, ws_ref, wn_ref, cot_ref, hid_ref, final,
-    feat, listed, via, turned, asked, rows_of, index, dest, table, near, outgoing, landed, choose, held, dense, ring, ringed,
+    feat, stacked, spots, listed, via, turned, asked, rows_of, index, dest, table, near, outgoing, landed, choose, held, dense, ring, ringed,
     rows, part, part_out, got_part, slopes, grads, got_core, full, full_out, got_z, got_y,
     e_sem, a_send, a_recv, b_send, b_recv, i_sem, f_send, f_recv, o_sem, r_send, r_recv,
     x_send, x_recv, s_send, s_recv, c_send, c_recv, z_send, z_recv, y_send, y_recv, g_send, g_recv, d_send, d_recv,
@@ -100,7 +96,7 @@
     feat_copy.start()
     me = y * 2 + core
 
-    list_requests(own_ref, row_ref, listed)
+    list_requests(own_ref, row_ref, listed, stacked, spots)
     pl.semaphore_wait(barrier, len(targets))
     for k in range(1, NZ):
         remote(listed.at[lax.rem(z + k, NZ)], via.at[z], a_send.at[k - 1], a_recv.at[k - 1], near_z[k - 1]).start()
@@ -228,10 +224,17 @@
 
         ring_copy(step).start()
 
-    fetch(0)
+    def early(step, _):
+        fetch(step)
+        return 0
+
+    lax.fori_loop(0, 3, early, 0)
 
     def loop(step, _):
-        fetch(step + 1)
+        @pl.when(step < 5)
+        def _():
+            fetch(step + 3)
+
         gather_in(step)
         pass_on(step)
         return 0
@@ -354,6 +357,8 @@
         out_specs=(vmem, vmem),
         scratch_shapes=[
             pltpu.VMEM((192, 8192), bf16),
+            pltpu.VMEM((256, 8192), bf16),
+            pltpu.VMEM((256, 8192), bf16),
             pltpu.VMEM((8, 8, 256), i32),
             pltpu.VMEM((8, 8, 256), i32),
             pltpu.VMEM((8, 8, 256), i32),

time: 123 us -> 118 us (0.959)
  Pallas kernels: 123 us -> 117 us
    pallas_call x1, Pallas kernels: 121 us -> 115 us  [on_device(): pl.pallas_call(step_kernel, out_shape=(jax.ShapeDtypeStruct((128, 256), b...]
where the time goes in v4:
time: 118 us
  Pallas kernels  117 us (99%)
    pallas_call x1, Pallas kernels, on_device(): pl.pallas_call(step_kernel, out_shape=(jax.ShapeDtypeStruct((128, 256), b...  115 us

profile of v4, /device:TPU:1, one launch (start us, length us, event | category | flops | bytes accessed | tf_op | source)
XLA Modules:
  0.0 117.7 jit_solution(7802322100262356302)
XLA Ops:
  0.6 115.3 %step.1 = (bf16[128,256]{1,0:T(8,128)(2,1)}, bf16[2,8,24,256]{3,2,1,0:T(8,128)(2,1)}) custom-call(bf16[192,8192]{1,0:T(8,128)(2,1)} %feat_ref.1, s32[16,1,512]{2,1,0:T(1,128)} %bitcast.2, s32[16,512]{1,0:T(8,128)} %bitcast.3, bf16[192,256]{1,0:T(8,128)(2,1)} %ws_ref.1, bf16[192,256]{1,0:T(8,128)(2,1)} %wn_ref.1, bf16[128,256]{1,0:T(8,128)(2,1)} %cot_ref.1), custom_call_target="tpu_custom_call" | custom-call | tf_op jit(solution)/shard_map/step/pallas_call | solution.py:353
  115.9 1.7 %finish.1 = (bf16[128,256]{1,0:T(8,128)(2,1)}, f32[192,256]{1,0:T(8,128)}, f32[192,256]{1,0:T(8,128)}) custom-call(bf16[128,256]{1,0:T(8,128)(2,1)} %get-tuple-element.5.hid_ref, bf16[2,8,24,256]{3,2,1,0:T(8,128)(2,1)} %get-tuple-element.6.final_ref), custom_call_target="tpu_custom_call" | custom-call | tf_op jit(solution)/shard_map/finish/pallas_call | solution.py:400

commit v5 on v4

--- a/solution.py
+++ b/solution.py
@@ -67,18 +67,27 @@
     block = found[192:256]
     item = found[128:192] + 256 * (block - 1)
     target = jnp.where(block > 0, jnp.where(item < 512, item, 512 + (item & 511)), 1024)
-    listed[...] = (row + 8192 * target).reshape(8, 8, 256)
+    listed[...] = (row + 8192 * target).reshape(8, 8, 1, 256)
 
 
 def step_kernel(
     feat_ref, own_ref, row_ref, ws_ref, wn_ref, cot_ref, hid_ref, final,
-    feat, stacked, spots, listed, via, turned, asked, rows_of, index, dest, table, near, outgoing, landed, choose, held, dense, ring, ringed,
-    rows, part, part_out, got_part, slopes, grads, got_core, full, full_out, got_z, got_y,
+    feat, stacked, spots, listed, via, asked, rows_of, index, dest, table, near, outgoing, landed, choose, held, dense, ring, ringed,
+    rows, part, part_out, got_part, slopes, flat, grads, got_core, full, full_out, got_z,
     e_sem, a_send, a_recv, b_send, b_recv, i_sem, f_send, f_recv, o_sem, r_send, r_recv,
-    x_send, x_recv, s_send, s_recv, c_send, c_recv, z_send, z_recv, y_send, y_recv, g_send, g_recv, d_send, d_recv,
+    x_send, x_recv, s_send, s_recv, c_send, c_recv, z_send, z_recv, g_send, g_recv, d_send, d_recv,
 ):
     y, z, core, x = place()
-    near_z = [{"wide": wide_at(y, lax.rem(z + k, NZ), core), "narrow": x} for k in range(1, NZ)]
+    ys = [y] + [lax.rem(y + k, NY) for k in range(1, NY)]
+    zs = [z] + [lax.rem(z + k, NZ) for k in range(1, NZ)]
+    seats = [core, 1 - core]
+    everyone = [(dy, dz, dc) for dy in range(NY) for dz in range(NZ) for dc in range(2) if dy + dz + dc > 0]
+    column = [(dy, dz) for dy in range(NY) for dz in range(NZ) if dy + dz > 0]
+
+    def at(dy, dz, dc):
+        return {"wide": wide_at(ys[dy], zs[dz], seats[dc]), "narrow": x}
+
+    near_z = [at(0, k, 0) for k in range(1, NZ)]
     near_x = [{"wide": wide_at(y, z, core), "narrow": lax.rem(x + k, NX)} for k in range(1, NX)]
 
     def plane(q):
@@ -89,7 +98,7 @@
         return {"wide": wide_at(there, z, seat), "narrow": x}
 
     barrier = pltpu.get_barrier_semaphore()
-    targets = near_z + [plane_at(q) for q in range(1, 8)] + near_x
+    targets = [at(*peer) for peer in everyone] + near_x
     for target in targets:
         pl.semaphore_signal(barrier, inc=1, device_id=target, device_id_type=pl.DeviceIdType.MESH)
     feat_copy = pltpu.make_async_copy(feat_ref, feat, e_sem)
@@ -98,8 +107,14 @@
 
     list_requests(own_ref, row_ref, listed, stacked, spots)
     pl.semaphore_wait(barrier, len(targets))
+    for dy, dz, dc in everyone:
+        remote(
+            listed.at[zs[dz], ys[dy] * 2 + seats[dc]], asked.at[me, z],
+            b_send.at[dy * 16 + dz * 2 + dc], b_recv.at[dy * 16 + dz * 2 + dc], at(dy, dz, dc),
+        ).start()
     for k in range(1, NZ):
-        remote(listed.at[lax.rem(z + k, NZ)], via.at[z], a_send.at[k - 1], a_recv.at[k - 1], near_z[k - 1]).start()
+        remote(listed.at[zs[k]], via.at[z], a_send.at[k - 1], a_recv.at[k - 1], near_z[k - 1]).start()
+    asked[me, z] = listed[z, me]
     via[z] = listed[z]
 
     eye = (
@@ -116,29 +131,12 @@
         return 0
 
     feat_copy.wait()
-    lax.fori_loop(0, 16, turn, 0)
-    for k in range(1, NZ):
-        remote(listed.at[z], via.at[lax.rem(z + NZ - k, NZ)], a_send.at[k - 1], a_recv.at[k - 1], near_z[k - 1]).wait_recv()
-    for group in range(8):
-        for owner in range(8):
-            turned[owner, group:group + 1] = via[group, owner:owner + 1]
-
-    def tell(q, _):
-        there, seat = plane(q)
-        remote(turned.at[there * 2 + seat], asked.at[me], b_send.at[q], b_recv.at[q], plane_at(q)).start()
-        return 0
-
-    lax.fori_loop(1, 8, tell, 0)
-    asked[me] = turned[me]
-    for owner in range(8):
-        dest[:, owner * 192:(owner + 1) * 192] = turned[owner][:, :192] >> 13
-    lax.fori_loop(16, 32, turn, 0)
-
-    def told(q, _):
-        remote(turned.at[0], asked.at[0], b_send.at[q], b_recv.at[q], plane_at(q)).wait_recv()
-        return 0
-
-    lax.fori_loop(1, 8, told, 0)
+    lax.fori_loop(0, 32, turn, 0)
+    for dy, dz, dc in everyone:
+        remote(
+            listed.at[z, me], asked.at[me, z],
+            b_send.at[dy * 16 + dz * 2 + dc], b_recv.at[dy * 16 + dz * 2 + dc], at(dy, dz, dc),
+        ).wait_recv()
     rows_of[...] = 2 * (asked[...] & 8191).reshape(64, 256)
     copy = pltpu.make_async_copy(rows_of, index, i_sem)
     copy.start()
@@ -229,6 +227,10 @@
         return 0
 
     lax.fori_loop(0, 3, early, 0)
+    for k in range(1, NZ):
+        remote(listed.at[z], via.at[lax.rem(z + NZ - k, NZ)], a_send.at[k - 1], a_recv.at[k - 1], near_z[k - 1]).wait_recv()
+    for owner in range(8):
+        dest[:, owner * 192:(owner + 1) * 192] = via[:, owner].reshape(8, 256)[:, :192] >> 13
 
     def loop(step, _):
         @pl.when(step < 5)
@@ -278,37 +280,44 @@
     hid_ref[...] = (0.5 * value * (1.0 + bend)).astype(jnp.bfloat16)
     for k in range(1, NX):
         remote(slopes.at[x], slopes.at[lax.rem(x + NX - k, NX)], s_send.at[k - 1], s_recv.at[k - 1], near_x[k - 1]).wait_recv()
-    grads[...] = lax.dot_general(
+    flat[...] = lax.dot_general(
         rows[...], slopes[...].reshape(512, 256), (((0,), (0,)), ((), ())), preferred_element_type=jnp.float32
-    ).reshape(2, NZ, 24, 256)
+    )
+    for half in range(2):
+        for piece in range(32):
+            grads[half, piece] = flat[half * 192 + piece * 6:half * 192 + piece * 6 + 6]
     copy = remote(grads.at[1 - core], got_core, c_send, c_recv, plane_at(1))
     copy.start()
     sent.append(copy)
     copy.wait_recv()
     full[...] = grads[core] + got_core[...]
     full_out[...] = full[...].astype(jnp.bfloat16)
-    for k in range(1, NZ):
-        copy = remote(full_out.at[lax.rem(z + k, NZ)], got_z.at[k - 1], z_send.at[k - 1], z_recv.at[k - 1], near_z[k - 1])
+    spot = y * NZ + z
+    for dy, dz in column:
+        copy = remote(
+            full_out.at[ys[dy] * NZ + zs[dz]], got_z.at[dy * NZ + dz],
+            z_send.at[dy * NZ + dz], z_recv.at[dy * NZ + dz], at(dy, dz, 0),
+        )
         copy.start()
         sent.append(copy)
-    mine = full[z]
-    for k in range(1, NZ):
-        remote(full_out.at[z], got_z.at[k - 1], z_send.at[k - 1], z_recv.at[k - 1], near_z[k - 1]).wait_recv()
-        mine = mine + got_z[k - 1].astype(jnp.float32)
-    got_y[y] = mine
-    for k in range(1, NY):
-        copy = remote(got_y.at[y], got_y.at[y], y_send.at[k - 1], y_recv.at[k - 1], plane_at(2 * k))
+    mine = full[spot]
+    for dy, dz in column:
+        remote(
+            full_out.at[spot], got_z.at[dy * NZ + dz], z_send.at[dy * NZ + dz], z_recv.at[dy * NZ + dz], at(dy, dz, 0)
+        ).wait_recv()
+        mine = mine + got_z[dy * NZ + dz].astype(jnp.float32)
+    final[core, spot] = mine.astype(jnp.bfloat16)
+    for dy, dz in column:
+        copy = remote(
+            final.at[core, spot], final.at[core, spot], g_send.at[dy * NZ + dz], g_recv.at[dy * NZ + dz], at(dy, dz, 0)
+        )
         copy.start()
         sent.append(copy)
-    for k in range(1, NY):
-        remote(got_y.at[y], got_y.at[lax.rem(y + NY - k, NY)], y_send.at[k - 1], y_recv.at[k - 1], plane_at(2 * k)).wait_recv()
-    final[core, z] = (got_y[0] + got_y[1] + got_y[2] + got_y[3]).astype(jnp.bfloat16)
-    for k in range(1, NZ):
-        copy = remote(final.at[core, z], final.at[core, z], g_send.at[k - 1], g_recv.at[k - 1], near_z[k - 1])
-        copy.start()
-        sent.append(copy)
-    for k in range(1, NZ):
-        remote(final.at[core, z], final.at[core, lax.rem(z + NZ - k, NZ)], g_send.at[k - 1], g_recv.at[k - 1], near_z[k - 1]).wait_recv()
+    for dy, dz in column:
+        there = ys[(NY - dy) % NY] * NZ + zs[(NZ - dz) % NZ]
+        remote(
+            final.at[core, spot], final.at[core, there], g_send.at[dy * NZ + dz], g_recv.at[dy * NZ + dz], at(dy, dz, 0)
+        ).wait_recv()
     copy = remote(final.at[core], final.at[core], d_send, d_recv, plane_at(1))
     copy.start()
     sent.append(copy)
@@ -319,9 +328,13 @@
     for k in range(1, NZ):
         remote(listed.at[z], via.at[z], a_send.at[k - 1], a_recv.at[k - 1], near_z[k - 1]).wait_send()
 
+    for dy, dz, dc in everyone:
+        remote(
+            listed.at[z, me], asked.at[me, z],
+            b_send.at[dy * 16 + dz * 2 + dc], b_recv.at[dy * 16 + dz * 2 + dc], at(dy, dz, dc),
+        ).wait_send()
+
     def drain(q, _):
-        remote(turned.at[0], asked.at[0], b_send.at[q], b_recv.at[q], plane_at(q)).wait_send()
-
         def each(step, _):
             remote(outgoing.at[step, q], landed.at[step, me], f_send.at[step, q], f_recv.at[step, q], plane_at(q)).wait_send()
             return 0
@@ -340,10 +353,15 @@
 
 def finish_kernel(hid_ref, final_ref, out_ref, gs_ref, gn_ref):
     out_ref[...] = hid_ref[...]
-    whole = final_ref[...].astype(jnp.float32).reshape(384, 256)
-    gs_ref[...] = whole[:192]
-    gn_ref[0:128] = whole[256:]
-    gn_ref[128:192] = whole[192:256]
+    for piece in range(32):
+        first = piece * 6
+        gs_ref[first:first + 6] = final_ref[0, piece].astype(jnp.float32)
+        block = final_ref[1, piece].astype(jnp.float32)
+        low = min(6, max(0, 64 - first))
+        if low > 0:
+            gn_ref[128 + first:128 + first + low] = block[:low]
+        if low < 6:
+            gn_ref[first + low - 64:first - 58] = block[low:]
 
 
 def on_device(features, owner_of, row_of, w_self, w_neighbor, cotangent):
@@ -352,17 +370,16 @@
     f32, bf16, i32 = jnp.float32, jnp.bfloat16, jnp.int32
     hidden, final = pl.pallas_call(
         step_kernel,
-        out_shape=(jax.ShapeDtypeStruct((128, 256), bf16), jax.ShapeDtypeStruct((2, NZ, 24, 256), bf16)),
+        out_shape=(jax.ShapeDtypeStruct((128, 256), bf16), jax.ShapeDtypeStruct((2, 32, 6, 256), bf16)),
         in_specs=[pl.BlockSpec(memory_space=pl.ANY)] + [vmem] * 5,
         out_specs=(vmem, vmem),
         scratch_shapes=[
             pltpu.VMEM((192, 8192), bf16),
             pltpu.VMEM((256, 8192), bf16),
             pltpu.VMEM((256, 8192), bf16),
-            pltpu.VMEM((8, 8, 256), i32),
-            pltpu.VMEM((8, 8, 256), i32),
-            pltpu.VMEM((8, 8, 256), i32),
-            pltpu.VMEM((8, 8, 256), i32),
+            pltpu.VMEM((8, 8, 1, 256), i32),
+            pltpu.VMEM((8, 8, 1, 256), i32),
+            pltpu.VMEM((8, 8, 1, 256), i32),
             pltpu.VMEM((64, 256), i32),
             pltpu.SMEM((64, 256), i32),
             pltpu.VMEM((8, 1536), i32),
@@ -380,17 +397,16 @@
             pltpu.VMEM((NX, 128, 256), bf16),
             pltpu.VMEM((NX - 1, 128, 256), bf16),
             pltpu.VMEM((NX, 128, 256), bf16),
-            pltpu.VMEM((2, NZ, 24, 256), f32),
-            pltpu.VMEM((NZ, 24, 256), f32),
-            pltpu.VMEM((NZ, 24, 256), f32),
-            pltpu.VMEM((NZ, 24, 256), bf16),
-            pltpu.VMEM((NZ - 1, 24, 256), bf16),
-            pltpu.VMEM((NY, 24, 256), f32),
-            dma(()), dma((NZ - 1,)), dma((NZ - 1,)), dma((8,)), dma((8,)), dma(()),
+            pltpu.VMEM((384, 256), f32),
+            pltpu.VMEM((2, 32, 6, 256), f32),
+            pltpu.VMEM((32, 6, 256), f32),
+            pltpu.VMEM((32, 6, 256), f32),
+            pltpu.VMEM((32, 6, 256), bf16),
+            pltpu.VMEM((32, 6, 256), bf16),
+            dma(()), dma((NZ - 1,)), dma((NZ - 1,)), dma((64,)), dma((64,)), dma(()),
             dma((8, 8)), dma((8, 8)), dma((8,)), dma((7,)), dma((7,)),
             dma((NX - 1,)), dma((NX - 1,)), dma((NX - 1,)), dma((NX - 1,)), dma(()), dma(()),
-            dma((NZ - 1,)), dma((NZ - 1,)), dma((NY - 1,)), dma((NY - 1,)),
-            dma((NZ - 1,)), dma((NZ - 1,)), dma(()), dma(()),
+            dma((32,)), dma((32,)), dma((32,)), dma((32,)), dma(()), dma(()),
         ],
         compiler_params=pltpu.CompilerParams(
             collective_id=1, has_side_effects=True, vmem_limit_bytes=60 * 1024 * 1024

time: 118 us -> 120 us (1.017)
  Pallas kernels: 117 us -> 119 us
    pallas_call x1, Pallas kernels: 115 us -> 117 us  [on_device(): pl.pallas_call(step_kernel, out_shape=(jax.ShapeDtypeStruct((128, 256), b...]
where the time goes in v5:
time: 120 us; the launch traced here: 119 us
  Pallas kernels  119 us (99%)
    pallas_call x1, Pallas kernels, on_device(): pl.pallas_call(step_kernel, out_shape=(jax.ShapeDtypeStruct((128, 256), b...  117 us

profile of v5, /device:TPU:1, one launch (start us, length us, event | category | flops | bytes accessed | tf_op | source)
XLA Modules:
  0.0 119.4 jit_solution(2644686436420155983)
XLA Ops:
  0.6 117.0 %step.1 = (bf16[128,256]{1,0:T(8,128)(2,1)}, bf16[2,32,6,256]{3,2,1,0:T(8,128)(2,1)}) custom-call(bf16[192,8192]{1,0:T(8,128)(2,1)} %feat_ref.1, s32[16,1,512]{2,1,0:T(1,128)} %bitcast.2, s32[16,512]{1,0:T(8,128)} %bitcast.3, bf16[192,256]{1,0:T(8,128)(2,1)} %ws_ref.1, bf16[192,256]{1,0:T(8,128)(2,1)} %wn_ref.1, bf16[128,256]{1,0:T(8,128)(2,1)} %cot_ref.1), custom_call_target="tpu_custom_call" | custom-call | tf_op jit(solution)/shard_map/step/pallas_call | solution.py:371
  117.6 1.8 %finish.1 = (bf16[128,256]{1,0:T(8,128)(2,1)}, f32[192,256]{1,0:T(8,128)}, f32[192,256]{1,0:T(8,128)}) custom-call(bf16[128,256]{1,0:T(8,128)(2,1)} %get-tuple-element.5.hid_ref, bf16[2,32,6,256]{3,2,1,0:T(8,128)(2,1)} %get-tuple-element.6.final_ref), custom_call_target="tpu_custom_call" | custom-call | tf_op jit(solution)/shard_map/finish/pallas_call | solution.py:416

commit v6 on v4

--- a/solution.py
+++ b/solution.py
@@ -40,8 +40,7 @@
         lax.broadcasted_iota(jnp.int32, (512, 512), 0) < lax.broadcasted_iota(jnp.int32, (512, 512), 1)
     ).astype(jnp.float32).astype(jnp.bfloat16)
     owner_id = lax.broadcasted_iota(jnp.int32, (64, 512), 0)
-    slot_id = lax.broadcasted_iota(jnp.int32, (256, 512), 0)
-    slot_id = jnp.where(slot_id < 192, slot_id, slot_id - 64)
+    slot_id = lax.broadcasted_iota(jnp.int32, (192, 512), 0)
     lane = lax.broadcasted_iota(jnp.int32, (1, 512), 1)
 
     def one(j, used):
@@ -50,12 +49,13 @@
         place_of = ((owner >> 1) & 7) * 8 + (owner >> 4) * 2 + (owner & 1)
         mine = owner_id == place_of
         onehot = jnp.where(mine, 1.0, 0.0)
-        within = jnp.dot(onehot.astype(jnp.bfloat16), upper, preferred_element_type=jnp.float32)
+        short = onehot.astype(jnp.bfloat16)
+        within = jnp.dot(short, upper, preferred_element_type=jnp.float32)
         slot = jnp.sum(onehot * (within + used), axis=0, keepdims=True).astype(jnp.int32)
         span = pl.ds(pl.multiple_of(j * 512, 512), 512)
         spots[:, span] = jnp.where(slot_id == slot, 1.0, 0.0).astype(jnp.bfloat16)
         for i, piece in enumerate([row & 255, row >> 8, lane & 255, (lane >> 8) + 2 * j + 1]):
-            stacked[i * 64:(i + 1) * 64, span] = jnp.where(mine, piece.astype(jnp.float32), 0.0).astype(jnp.bfloat16)
+            stacked[i * 64:(i + 1) * 64, span] = short * piece.astype(jnp.float32).astype(jnp.bfloat16)
         return used + jnp.sum(onehot, axis=1, keepdims=True)
 
     lax.fori_loop(0, 16, one, jnp.zeros((64, 1), jnp.float32))
@@ -67,7 +67,8 @@
     block = found[192:256]
     item = found[128:192] + 256 * (block - 1)
     target = jnp.where(block > 0, jnp.where(item < 512, item, 512 + (item & 511)), 1024)
-    listed[...] = (row + 8192 * target).reshape(8, 8, 256)
+    listed[...] = jnp.zeros_like(listed)
+    listed[:, :, 0:192] = (row + 8192 * target).reshape(8, 8, 192)
 
 
 def step_kernel(
@@ -150,7 +151,9 @@
     def fetch(step):
         group = lax.rem(z + order_of(step), NZ)
 
-        def one(q, _):
+        def one(i, _):
+            turn_of = lax.rem(i, 3)
+            q = jnp.where(i < 6, 2 * jnp.where(turn_of == 2, 1, 2 + turn_of) + i // 3, 7 - i)
             there, seat = plane(q)
             line = (there * 2 + seat) * 8 + group
 
@@ -252,32 +255,42 @@
         rows[:, i * 128:(i + 1) * 128] = total.astype(jnp.bfloat16)
 
     middle = jnp.concatenate([ws_ref[128:192], wn_ref[128:192]], axis=0)
-    for k in range(NX):
-        span = slice(k * 128, (k + 1) * 128)
+    def project(k):
+        span = pl.ds(pl.multiple_of(lax.rem(x + k, NX) * 128, 128), 128)
         value = jnp.dot(rows[span, 0:128], ws_ref[0:128], preferred_element_type=jnp.float32)
         value = value + jnp.dot(rows[span, 128:256], middle, preferred_element_type=jnp.float32)
         value = value + jnp.dot(rows[span, 256:384], wn_ref[0:128], preferred_element_type=jnp.float32)
-        part[k] = value
-        part_out[k] = value.astype(jnp.bfloat16)
+        return value.reshape(2, 64, 256)
+
+    def part_copy(k, h):
+        return remote(part_out.at[k - 1, h], got_part.at[k - 1, h], x_send.at[k - 1, h], x_recv.at[k - 1, h], near_x[k - 1])
+
     sent = []
+    for k in (2, 1, 3):
+        part_out[k - 1] = project(k).astype(jnp.bfloat16)
+        part_copy(k, 0).start()
+    for k in (2, 1, 3):
+        part_copy(k, 1).start()
+        sent += [part_copy(k, 0), part_copy(k, 1)]
+    part[...] = project(0)
+    for h in range(2):
+        value = part[h]
+        for k in range(1, NX):
+            part_copy(k, h).wait_recv()
+            value = value + got_part[k - 1, h].astype(jnp.float32)
+        bend = jnp.tanh(ROOT * (value + CUBE * value * value * value))
+        rise = 0.5 * (1.0 + bend) + 0.5 * value * (1.0 - bend * bend) * ROOT * (1.0 + 3.0 * CUBE * value * value)
+        slopes[x, h] = (cot_ref[h * 64:(h + 1) * 64].astype(jnp.float32) * rise).astype(jnp.bfloat16)
+        for k in (2, 1, 3):
+            copy = remote(slopes.at[x, h], slopes.at[x, h], s_send.at[k - 1, h], s_recv.at[k - 1, h], near_x[k - 1])
+            copy.start()
+            sent.append(copy)
+        hid_ref[h * 64:(h + 1) * 64] = (0.5 * value * (1.0 + bend)).astype(jnp.bfloat16)
     for k in range(1, NX):
-        copy = remote(part_out.at[lax.rem(x + k, NX)], got_part.at[k - 1], x_send.at[k - 1], x_recv.at[k - 1], near_x[k - 1])
-        copy.start()
-        sent.append(copy)
-    value = part[x]
-    for k in range(1, NX):
-        sent[k - 1].wait_recv()
-        value = value + got_part[k - 1].astype(jnp.float32)
-    bend = jnp.tanh(ROOT * (value + CUBE * value * value * value))
-    rise = 0.5 * (1.0 + bend) + 0.5 * value * (1.0 - bend * bend) * ROOT * (1.0 + 3.0 * CUBE * value * value)
-    slopes[x] = (cot_ref[...].astype(jnp.float32) * rise).astype(jnp.bfloat16)
-    for k in range(1, NX):
-        copy = remote(slopes.at[x], slopes.at[x], s_send.at[k - 1], s_recv.at[k - 1], near_x[k - 1])
-        copy.start()
-        sent.append(copy)
-    hid_ref[...] = (0.5 * value * (1.0 + bend)).astype(jnp.bfloat16)
-    for k in range(1, NX):
-        remote(slopes.at[x], slopes.at[lax.rem(x + NX - k, NX)], s_send.at[k - 1], s_recv.at[k - 1], near_x[k - 1]).wait_recv()
+        for h in range(2):
+            remote(
+                slopes.at[x, h], slopes.at[lax.rem(x + NX - k, NX), h], s_send.at[k - 1, h], s_recv.at[k - 1, h], near_x[k - 1]
+            ).wait_recv()
     grads[...] = lax.dot_general(
         rows[...], slopes[...].reshape(512, 256), (((0,), (0,)), ((), ())), preferred_element_type=jnp.float32
     ).reshape(2, NZ, 24, 256)
@@ -307,12 +320,16 @@
         copy = remote(final.at[core, z], final.at[core, z], g_send.at[k - 1], g_recv.at[k - 1], near_z[k - 1])
         copy.start()
         sent.append(copy)
-    for k in range(1, NZ):
-        remote(final.at[core, z], final.at[core, lax.rem(z + NZ - k, NZ)], g_send.at[k - 1], g_recv.at[k - 1], near_z[k - 1]).wait_recv()
-    copy = remote(final.at[core], final.at[core], d_send, d_recv, plane_at(1))
-    copy.start()
-    sent.append(copy)
-    remote(final.at[core], final.at[1 - core], d_send, d_recv, plane_at(1)).wait_recv()
+    for k in range(NZ):
+        there = lax.rem(z + NZ - k, NZ)
+        if k > 0:
+            remote(final.at[core, z], final.at[core, there], g_send.at[k - 1], g_recv.at[k - 1], near_z[k - 1]).wait_recv()
+        copy = remote(final.at[core, there], final.at[core, there], d_send.at[k], d_recv.at[k], plane_at(1))
+        copy.start()
+        sent.append(copy)
+    for k in range(NZ):
+        there = lax.rem(z + NZ - k, NZ)
+        remote(final.at[core, z], final.at[1 - core, there], d_send.at[k], d_recv.at[k], plane_at(1)).wait_recv()
     for copy in sent:
         copy.wait_send()
 
@@ -358,7 +375,7 @@
         scratch_shapes=[
             pltpu.VMEM((192, 8192), bf16),
             pltpu.VMEM((256, 8192), bf16),
-            pltpu.VMEM((256, 8192), bf16),
+            pltpu.VMEM((192, 8192), bf16),
             pltpu.VMEM((8, 8, 256), i32),
             pltpu.VMEM((8, 8, 256), i32),
             pltpu.VMEM((8, 8, 256), i32),
@@ -376,10 +393,10 @@
             pltpu.VMEM((7, 3, 512, 128), bf16),
             pltpu.VMEM((7, 3, 512, 128), bf16),
             pltpu.VMEM((512, 384), bf16),
-            pltpu.VMEM((NX, 128, 256), f32),
-            pltpu.VMEM((NX, 128, 256), bf16),
-            pltpu.VMEM((NX - 1, 128, 256), bf16),
-            pltpu.VMEM((NX, 128, 256), bf16),
+            pltpu.VMEM((2, 64, 256), f32),
+            pltpu.VMEM((NX - 1, 2, 64, 256), bf16),
+            pltpu.VMEM((NX - 1, 2, 64, 256), bf16),
+            pltpu.VMEM((NX, 2, 64, 256), bf16),
             pltpu.VMEM((2, NZ, 24, 256), f32),
             pltpu.VMEM((NZ, 24, 256), f32),
             pltpu.VMEM((NZ, 24, 256), f32),
@@ -388,9 +405,9 @@
             pltpu.VMEM((NY, 24, 256), f32),
             dma(()), dma((NZ - 1,)), dma((NZ - 1,)), dma((8,)), dma((8,)), dma(()),
             dma((8, 8)), dma((8, 8)), dma((8,)), dma((7,)), dma((7,)),
-            dma((NX - 1,)), dma((NX - 1,)), dma((NX - 1,)), dma((NX - 1,)), dma(()), dma(()),
+            dma((NX - 1, 2)), dma((NX - 1, 2)), dma((NX - 1, 2)), dma((NX - 1, 2)), dma(()), dma(()),
             dma((NZ - 1,)), dma((NZ - 1,)), dma((NY - 1,)), dma((NY - 1,)),
-            dma((NZ - 1,)), dma((NZ - 1,)), dma(()), dma(()),
+            dma((NZ - 1,)), dma((NZ - 1,)), dma((NZ,)), dma((NZ,)),
         ],
         compiler_params=pltpu.CompilerParams(
             collective_id=1, has_side_effects=True, vmem_limit_bytes=60 * 1024 * 1024

time: 118 us -> 116 us (0.983)
  Pallas kernels: 117 us -> 115 us
    pallas_call x1, Pallas kernels: 115 us -> 113 us  [on_device(): pl.pallas_call(step_kernel, out_shape=(jax.ShapeDtypeStruct((128, 256), b...]
where the time goes in v6:
time: 116 us
  Pallas kernels  115 us (99%)
    pallas_call x1, Pallas kernels, on_device(): pl.pallas_call(step_kernel, out_shape=(jax.ShapeDtypeStruct((128, 256), b...  113 us

profile of v6, /device:TPU:1, one launch (start us, length us, event | category | flops | bytes accessed | tf_op | source)
XLA Modules:
  0.0 115.9 jit_solution(12233044976347591928)
XLA Ops:
  0.6 113.5 %step.1 = (bf16[128,256]{1,0:T(8,128)(2,1)}, bf16[2,8,24,256]{3,2,1,0:T(8,128)(2,1)}) custom-call(bf16[192,8192]{1,0:T(8,128)(2,1)} %feat_ref.1, s32[16,1,512]{2,1,0:T(1,128)} %bitcast.2, s32[16,512]{1,0:T(8,128)} %bitcast.3, bf16[192,256]{1,0:T(8,128)(2,1)} %ws_ref.1, bf16[192,256]{1,0:T(8,128)(2,1)} %wn_ref.1, bf16[128,256]{1,0:T(8,128)(2,1)} %cot_ref.1), custom_call_target="tpu_custom_call" | custom-call | tf_op jit(solution)/shard_map/step/pallas_call | solution.py:370
  114.1 1.7 %finish.1 = (bf16[128,256]{1,0:T(8,128)(2,1)}, f32[192,256]{1,0:T(8,128)}, f32[192,256]{1,0:T(8,128)}) custom-call(bf16[128,256]{1,0:T(8,128)(2,1)} %get-tuple-element.5.hid_ref, bf16[2,8,24,256]{3,2,1,0:T(8,128)(2,1)} %get-tuple-element.6.final_ref), custom_call_target="tpu_custom_call" | custom-call | tf_op jit(solution)/shard_map/finish/pallas_call | solution.py:417

commit v7 on v6

--- a/solution.py
+++ b/solution.py
@@ -37,7 +37,7 @@
 
 def list_requests(own_ref, row_ref, listed, stacked, spots):
     upper = (
-        lax.broadcasted_iota(jnp.int32, (512, 512), 0) < lax.broadcasted_iota(jnp.int32, (512, 512), 1)
+        lax.broadcasted_iota(jnp.int32, (256, 256), 0) < lax.broadcasted_iota(jnp.int32, (256, 256), 1)
     ).astype(jnp.float32).astype(jnp.bfloat16)
     owner_id = lax.broadcasted_iota(jnp.int32, (64, 512), 0)
     slot_id = lax.broadcasted_iota(jnp.int32, (192, 512), 0)
@@ -50,15 +50,19 @@
         mine = owner_id == place_of
         onehot = jnp.where(mine, 1.0, 0.0)
         short = onehot.astype(jnp.bfloat16)
-        within = jnp.dot(short, upper, preferred_element_type=jnp.float32)
-        slot = jnp.sum(onehot * (within + used), axis=0, keepdims=True).astype(jnp.int32)
+        within = jnp.dot(
+            jnp.concatenate([short[:, :256], short[:, 256:]], axis=0), upper, preferred_element_type=jnp.float32
+        )
+        half = used + jnp.sum(onehot[:, :256], axis=1, keepdims=True)
+        before = jnp.concatenate([within[:64] + used, within[64:] + half], axis=1)
+        slot = jnp.sum(onehot * before, axis=0, keepdims=True).astype(jnp.int32)
         span = pl.ds(pl.multiple_of(j * 512, 512), 512)
         spots[:, span] = jnp.where(slot_id == slot, 1.0, 0.0).astype(jnp.bfloat16)
         for i, piece in enumerate([row & 255, row >> 8, lane & 255, (lane >> 8) + 2 * j + 1]):
             stacked[i * 64:(i + 1) * 64, span] = short * piece.astype(jnp.float32).astype(jnp.bfloat16)
-        return used + jnp.sum(onehot, axis=1, keepdims=True)
-
-    lax.fori_loop(0, 16, one, jnp.zeros((64, 1), jnp.float32))
+        return half + jnp.sum(onehot[:, 256:], axis=1, keepdims=True)
+
+    lax.fori_loop(0, 16, one, jnp.zeros((64, 1), jnp.float32), unroll=4)
     found = lax.dot_general(
         stacked[...], spots[...], (((1,), (1,)), ((), ())), preferred_element_type=jnp.float32
     )
@@ -140,22 +144,33 @@
         return 0
 
     lax.fori_loop(1, 8, told, 0)
-    rows_of[...] = 2 * (asked[...] & 8191).reshape(64, 256)
-    copy = pltpu.make_async_copy(rows_of, index, i_sem)
-    copy.start()
-    copy.wait()
+    for group in range(8):
+        rows_of[group] = 2 * (asked[:, group] & 8191)
+
+    def index_copy(step):
+        group = lax.rem(z + order_of(step), NZ)
+        return pltpu.make_async_copy(
+            rows_of.at[group], index.at[pl.ds(pl.multiple_of(group * 8, 8), 8)], i_sem.at[step]
+        )
+
+    def take(step, _):
+        index_copy(step).start()
+        return 0
+
+    lax.fori_loop(0, 8, take, 0)
 
     low_half = lax.broadcasted_iota(jnp.int32, (96, 128), 1) < 64
     low_lane = lax.broadcasted_iota(jnp.int32, (512, 128), 1) < 64
 
     def fetch(step):
         group = lax.rem(z + order_of(step), NZ)
+        index_copy(step).wait()
 
         def one(i, _):
             turn_of = lax.rem(i, 3)
             q = jnp.where(i < 6, 2 * jnp.where(turn_of == 2, 1, 2 + turn_of) + i // 3, 7 - i)
             there, seat = plane(q)
-            line = (there * 2 + seat) * 8 + group
+            line = group * 8 + there * 2 + seat
 
             for s in range(192):
                 near[2 * s:2 * s + 2, :] = table[pl.ds(index[line, s], 2), :]
@@ -380,7 +395,7 @@
             pltpu.VMEM((8, 8, 256), i32),
             pltpu.VMEM((8, 8, 256), i32),
             pltpu.VMEM((8, 8, 256), i32),
-            pltpu.VMEM((64, 256), i32),
+            pltpu.VMEM((8, 8, 256), i32),
             pltpu.SMEM((64, 256), i32),
             pltpu.VMEM((8, 1536), i32),
             pltpu.VMEM((16384, 128), f32),
@@ -403,7 +418,7 @@
             pltpu.VMEM((NZ, 24, 256), bf16),
             pltpu.VMEM((NZ - 1, 24, 256), bf16),
             pltpu.VMEM((NY, 24, 256), f32),
-            dma(()), dma((NZ - 1,)), dma((NZ - 1,)), dma((8,)), dma((8,)), dma(()),
+            dma(()), dma((NZ - 1,)), dma((NZ - 1,)), dma((8,)), dma((8,)), dma((8,)),
             dma((8, 8)), dma((8, 8)), dma((8,)), dma((7,)), dma((7,)),
             dma((NX - 1, 2)), dma((NX - 1, 2)), dma((NX - 1, 2)), dma((NX - 1, 2)), dma(()), dma(()),
             dma((NZ - 1,)), dma((NZ - 1,)), dma((NY - 1,)), dma((NY - 1,)),

time: 116 us -> 113 us (0.974)
  Pallas kernels: 115 us -> 112 us
    pallas_call x1, Pallas kernels: 113 us -> 110 us  [on_device(): pl.pallas_call(step_kernel, out_shape=(jax.ShapeDtypeStruct((128, 256), b...]
where the time goes in v7:
time: 113 us
  Pallas kernels  112 us (99%)
    pallas_call x1, Pallas kernels, on_device(): pl.pallas_call(step_kernel, out_shape=(jax.ShapeDtypeStruct((128, 256), b...  110 us

profile of v7, /device:TPU:1, one launch (start us, length us, event | category | flops | bytes accessed | tf_op | source)
XLA Modules:
  0.0 112.6 jit_solution(12486724195712796904)
XLA Ops:
  0.6 110.2 %step.1 = (bf16[128,256]{1,0:T(8,128)(2,1)}, bf16[2,8,24,256]{3,2,1,0:T(8,128)(2,1)}) custom-call(bf16[192,8192]{1,0:T(8,128)(2,1)} %feat_ref.1, s32[16,1,512]{2,1,0:T(1,128)} %bitcast.2, s32[16,512]{1,0:T(8,128)} %bitcast.3, bf16[192,256]{1,0:T(8,128)(2,1)} %ws_ref.1, bf16[192,256]{1,0:T(8,128)(2,1)} %wn_ref.1, bf16[128,256]{1,0:T(8,128)(2,1)} %cot_ref.1), custom_call_target="tpu_custom_call" | custom-call | tf_op jit(solution)/shard_map/step/pallas_call | solution.py:385
  110.9 1.7 %finish.1 = (bf16[128,256]{1,0:T(8,128)(2,1)}, f32[192,256]{1,0:T(8,128)}, f32[192,256]{1,0:T(8,128)}) custom-call(bf16[128,256]{1,0:T(8,128)(2,1)} %get-tuple-element.5.hid_ref, bf16[2,8,24,256]{3,2,1,0:T(8,128)(2,1)} %get-tuple-element.6.final_ref), custom_call_target="tpu_custom_call" | custom-call | tf_op jit(solution)/shard_map/finish/pallas_call | solution.py:432

commit v8 on v7

--- a/solution.py
+++ b/solution.py
@@ -78,7 +78,7 @@
 def step_kernel(
     feat_ref, own_ref, row_ref, ws_ref, wn_ref, cot_ref, hid_ref, final,
     feat, stacked, spots, listed, via, turned, asked, rows_of, index, dest, table, near, outgoing, landed, choose, held, dense, ring, ringed,
-    rows, part, part_out, got_part, slopes, grads, got_core, full, full_out, got_z, got_y,
+    rows, rows_turned, part, part_out, got_part, slopes, grads, got_core, full, full_out, got_z, got_y,
     e_sem, a_send, a_recv, b_send, b_recv, i_sem, f_send, f_recv, o_sem, r_send, r_recv,
     x_send, x_recv, s_send, s_recv, c_send, c_recv, z_send, z_recv, y_send, y_recv, g_send, g_recv, d_send, d_recv,
 ):
@@ -288,6 +288,7 @@
         part_copy(k, 1).start()
         sent += [part_copy(k, 0), part_copy(k, 1)]
     part[...] = project(0)
+    rows_turned[...] = rows[...].T
     for h in range(2):
         value = part[h]
         for k in range(1, NX):
@@ -306,8 +307,8 @@
             remote(
                 slopes.at[x, h], slopes.at[lax.rem(x + NX - k, NX), h], s_send.at[k - 1, h], s_recv.at[k - 1, h], near_x[k - 1]
             ).wait_recv()
-    grads[...] = lax.dot_general(
-        rows[...], slopes[...].reshape(512, 256), (((0,), (0,)), ((), ())), preferred_element_type=jnp.float32
+    grads[...] = jnp.dot(
+        rows_turned[...], slopes[...].reshape(512, 256), preferred_element_type=jnp.float32
     ).reshape(2, NZ, 24, 256)
     copy = remote(grads.at[1 - core], got_core, c_send, c_recv, plane_at(1))
     copy.start()
@@ -319,6 +320,27 @@
         copy = remote(full_out.at[lax.rem(z + k, NZ)], got_z.at[k - 1], z_send.at[k - 1], z_recv.at[k - 1], near_z[k - 1])
         copy.start()
         sent.append(copy)
+    for k in range(1, NZ):
+        remote(listed.at[z], via.at[z], a_send.at[k - 1], a_recv.at[k - 1], near_z[k - 1]).wait_send()
+
+    def drain(q, _):
+        remote(turned.at[0], asked.at[0], b_send.at[q], b_recv.at[q], plane_at(q)).wait_send()
+
+        def each(step, _):
+            remote(outgoing.at[step, q], landed.at[step, me], f_send.at[step, q], f_recv.at[step, q], plane_at(q)).wait_send()
+            return 0
+
+        lax.fori_loop(0, 8, each, 0)
+        return 0
+
+    lax.fori_loop(1, 8, drain, 0)
+
+    def drain_ring(step, _):
+        ring_copy(step).wait_send()
+        return 0
+
+    lax.fori_loop(0, 7, drain_ring, 0)
+
     mine = full[z]
     for k in range(1, NZ):
         remote(full_out.at[z], got_z.at[k - 1], z_send.at[k - 1], z_recv.at[k - 1], near_z[k - 1]).wait_recv()
@@ -347,27 +369,6 @@
         remote(final.at[core, z], final.at[1 - core, there], d_send.at[k], d_recv.at[k], plane_at(1)).wait_recv()
     for copy in sent:
         copy.wait_send()
-
-    for k in range(1, NZ):
-        remote(listed.at[z], via.at[z], a_send.at[k - 1], a_recv.at[k - 1], near_z[k - 1]).wait_send()
-
-    def drain(q, _):
-        remote(turned.at[0], asked.at[0], b_send.at[q], b_recv.at[q], plane_at(q)).wait_send()
-
-        def each(step, _):
-            remote(outgoing.at[step, q], landed.at[step, me], f_send.at[step, q], f_recv.at[step, q], plane_at(q)).wait_send()
-            return 0
-
-        lax.fori_loop(0, 8, each, 0)
-        return 0
-
-    lax.fori_loop(1, 8, drain, 0)
-
-    def drain_ring(step, _):
-        ring_copy(step).wait_send()
-        return 0
-
-    lax.fori_loop(0, 7, drain_ring, 0)
 
 
 def finish_kernel(hid_ref, final_ref, out_ref, gs_ref, gn_ref):
@@ -408,6 +409,7 @@
             pltpu.VMEM((7, 3, 512, 128), bf16),
             pltpu.VMEM((7, 3, 512, 128), bf16),
             pltpu.VMEM((512, 384), bf16),
+            pltpu.VMEM((384, 512), bf16),
             pltpu.VMEM((2, 64, 256), f32),
             pltpu.VMEM((NX - 1, 2, 64, 256), bf16),
             pltpu.VMEM((NX - 1, 2, 64, 256), bf16),

time: 113 us -> 112 us (level)
  no operation moved by 1% of the time
where the time goes in v8:
time: 112 us
  Pallas kernels  111 us (99%)
    pallas_call x1, Pallas kernels, on_device(): pl.pallas_call(step_kernel, out_shape=(jax.ShapeDtypeStruct((128, 256), b...  110 us

profile of v8, /device:TPU:1, one launch (start us, length us, event | category | flops | bytes accessed | tf_op | source)
XLA Modules:
  0.0 112.0 jit_solution(3542140425647219452)
XLA Ops:
  0.6 109.6 %step.1 = (bf16[128,256]{1,0:T(8,128)(2,1)}, bf16[2,8,24,256]{3,2,1,0:T(8,128)(2,1)}) custom-call(bf16[192,8192]{1,0:T(8,128)(2,1)} %feat_ref.1, s32[16,1,512]{2,1,0:T(1,128)} %bitcast.2, s32[16,512]{1,0:T(8,128)} %bitcast.3, bf16[192,256]{1,0:T(8,128)(2,1)} %ws_ref.1, bf16[192,256]{1,0:T(8,128)(2,1)} %wn_ref.1, bf16[128,256]{1,0:T(8,128)(2,1)} %cot_ref.1), custom_call_target="tpu_custom_call" | custom-call | tf_op jit(solution)/shard_map/step/pallas_call | solution.py:386
  110.3 1.7 %finish.1 = (bf16[128,256]{1,0:T(8,128)(2,1)}, f32[192,256]{1,0:T(8,128)}, f32[192,256]{1,0:T(8,128)}) custom-call(bf16[128,256]{1,0:T(8,128)(2,1)} %get-tuple-element.5.hid_ref, bf16[2,8,24,256]{3,2,1,0:T(8,128)(2,1)} %get-tuple-element.6.final_ref), custom_call_target="tpu_custom_call" | custom-call | tf_op jit(solution)/shard_map/finish/pallas_call | solution.py:434
